TPU v7x, 32 devices: a whole 2x2x4 slice. The times are simulated.
32 devices in a mesh: groups: 2 (over x), ctx: 4 (over y, core), head: 4 (over z).
Axes of the slice: x: 2, y: 2, z: 4, core: 2. Of those that a mesh axis runs over, the one named last changes fastest.
Arguments:
- hidden: bfloat16 [2, 2048, 4096], P(None, ('groups', 'ctx'), 'head'), parts along dimension 1, may hold values from -40 to 40
- strand_bases: int32 [2048], P(('groups', 'ctx')), parts along dimension 0, may hold values from 0 to 3
- variant_sites: int32 [256], P('groups'), parts along dimension 0, may hold values from 0 to 1023, as said below
- base_shift: int32 [256], P('groups'), parts along dimension 0, may hold values from 1 to 3
- base_embed: bfloat16 [4, 4096], replicated, may hold values from -6 to 6
- query_weight: bfloat16 [4096, 2048], P(None, 'head')
- key_weight: bfloat16 [4096, 2048], P(None, 'head')
- value_weight: bfloat16 [4096, 2048], P(None, 'head'), may hold values from -0.09375 to 0.09375
- out_weight: bfloat16 [2048, 4096], P('head'), may hold values from -4 to 4
Outputs:
- mixed: bfloat16 [2048, 4096], P(('groups', 'ctx'), 'head'), parts along dimension 0
There are 2 independent parts, one for each index of `groups`. A program takes and returns all parts, laid end to end along the dimension named above; an argument that names none is the same for every part. Nothing has to cross between parts.
Inputs may be any that keep to these rules, and one draw needn't show every extreme that they name: `variant_sites`: distinct positions; each aligned block of 256 positions holds at most 64 of them, and some block holds exactly that many.
All inputs are finite; a program needn't handle non-finite values.
Results may differ from a plain program's by a relative error of at most 0.019.
Values may be sent and summed in bfloat16 or wider, within the bound.
A program may use at most 128 MiB of HBM per device.

v0:
```python
import math

import jax
import jax.numpy as jnp
from jax import lax
from jax.sharding import PartitionSpec as P

HEAD_DIM = 128
VAR_DEV = 32


ROPE_BASE = 10000.0
NEG_FILL = -1e30


def rotate(values, positions):
    half_dim = values.shape[-1] // 2
    freq_table = jnp.power(
        ROPE_BASE, -jnp.arange(half_dim, dtype=jnp.float32) * 2.0 / values.shape[-1]
    )
    angle_grid = positions[:, None] * freq_table[None, :]
    cos_part = jnp.cos(angle_grid)[:, None, :]
    sin_part = jnp.sin(angle_grid)[:, None, :]
    lower_half = values[..., :half_dim]
    upper_half = values[..., half_dim:]
    return jnp.concatenate(
        [
            lower_half * cos_part - upper_half * sin_part,
            upper_half * cos_part + lower_half * sin_part,
        ],
        axis=-1,
    )


def project_all(inputs, query_weight, key_weight, value_weight, positions):
    n_rows = inputs.shape[0]
    heads_here = query_weight.shape[1] // HEAD_DIM

    def rotated(weight):
        product = jnp.dot(inputs, weight, preferred_element_type=jnp.float32)
        return (
            rotate(product.reshape(n_rows, heads_here, HEAD_DIM), positions)
            .reshape(n_rows, -1)
            .astype(jnp.bfloat16)
        )

    values_out = jnp.dot(inputs, value_weight, preferred_element_type=jnp.float32).astype(
        jnp.bfloat16
    )
    return (rotated(query_weight), rotated(key_weight), values_out)


def shards(
    hidden,
    strand_bases,
    variant_sites,
    base_shift,
    base_embed,
    query_weight,
    key_weight,
    value_weight,
    out_weight,
):
    row_count = hidden.shape[1]
    shard_total = lax.axis_size("ctx")
    window_rows = row_count * shard_total
    my_block = lax.axis_index("ctx")
    my_start = my_block * row_count
    slot_cap = 2 * VAR_DEV
    head_width = query_weight.shape[1]
    heads_here = head_width // HEAD_DIM
    score_scale = 1.0 / math.sqrt(HEAD_DIM)
    gathered = lax.all_gather(hidden, "head", axis=2, tiled=True)
    row_iota = jnp.arange(row_count, dtype=jnp.int32)
    query_pos = my_start + row_iota
    plus_pos = query_pos.astype(jnp.float32)
    minus_pos = (window_rows - 1 - query_pos).astype(jnp.float32)
    variant_count = variant_sites.shape[0]
    variant_iota = jnp.arange(variant_count, dtype=jnp.int32)
    variant_block = variant_sites // row_count
    same_block = (variant_block[:, None] == variant_block[None, :]) & (
        variant_iota[None, :] < variant_iota[:, None]
    )
    variant_rank = jnp.sum(same_block.astype(jnp.int32), axis=1)
    is_mine = variant_block == my_block
    slot_iota = jnp.arange(slot_cap, dtype=jnp.int32)
    slot_match = (variant_rank[:, None] == slot_iota[None, :]) & is_mine[:, None]
    row_match = ((variant_sites - my_start)[:, None] == row_iota[None, :]) & is_mine[:, None]
    selector_f = lax.dot_general(
        slot_match.astype(jnp.bfloat16),
        row_match.astype(jnp.bfloat16),
        (((0,), (0,)), ((), ())),
        preferred_element_type=jnp.float32,
    )
    selector = selector_f.astype(jnp.bfloat16)
    has_row = jnp.sum(selector_f, axis=0) > 0.5
    old_base = jnp.sum(jnp.where(row_match, strand_bases[None, :], 0), axis=1)
    new_base = jnp.mod(old_base + base_shift, 4)
    slot_old = jnp.sum(jnp.where(slot_match, old_base[:, None], 0), axis=0)
    slot_new = jnp.sum(jnp.where(slot_match, new_base[:, None], 0), axis=0)
    slot_pos = jnp.sum(jnp.where(slot_match, variant_sites[:, None], 0), axis=0)
    slot_live = jnp.sum(slot_match.astype(jnp.int32), axis=0) > 0
    embed_table = base_embed.astype(jnp.float32)
    code_iota = jnp.arange(4, dtype=jnp.int32)

    def embed_diff(new_codes, old_codes):
        onehot = (new_codes[:, None] == code_iota[None, :]).astype(jnp.float32) - (
            old_codes[:, None] == code_iota[None, :]
        ).astype(jnp.float32)
        onehot = jnp.where(slot_live[:, None], onehot, 0.0)
        return jnp.dot(onehot, embed_table, precision=lax.Precision.HIGHEST)

    def picked_rows(full_rows):
        return lax.dot_general(
            selector, full_rows, (((1,), (0,)), ((), ())), preferred_element_type=jnp.float32
        )

    mutant_rows_plus = (picked_rows(gathered[0]) + embed_diff(slot_new, slot_old)).astype(
        jnp.bfloat16
    )
    mutant_rows_minus = (picked_rows(gathered[1]) + embed_diff(3 - slot_new, 3 - slot_old)).astype(
        jnp.bfloat16
    )
    slot_plus_pos = slot_pos.astype(jnp.float32)
    slot_minus_pos = (window_rows - 1 - slot_pos).astype(jnp.float32)

    def spread(slot_rows, full_rows):
        placed = lax.dot_general(
            selector, slot_rows, (((0,), (0,)), ((), ())), preferred_element_type=jnp.float32
        )
        return jnp.where(has_row[:, None], placed.astype(jnp.bfloat16), full_rows)

    ref_plus = project_all(gathered[0], query_weight, key_weight, value_weight, plus_pos)
    ref_minus = project_all(gathered[1], query_weight, key_weight, value_weight, minus_pos)

    def strand_update(running, query_part, key_part, value_part, key_pos, forward):
        run_max, run_sum, run_vec = running
        scores = (
            jnp.einsum("sqhd,kshd->shqk", query_part, key_part, preferred_element_type=jnp.float32)
            * score_scale
        )
        if forward:
            allowed = key_pos[None, :] <= query_pos[:, None]
        else:
            allowed = key_pos[None, :] >= query_pos[:, None]
        masked = jnp.where(allowed, scores, NEG_FILL)
        new_max = jnp.maximum(run_max, jnp.max(masked, axis=-1))
        rescale = jnp.exp(run_max - new_max)
        weights = jnp.where(allowed, jnp.exp(scores - new_max[..., None]), 0.0)
        new_sum = rescale * run_sum + jnp.sum(weights, axis=-1)
        new_vec = rescale[..., None] * run_vec + jnp.einsum(
            "shqk,kshd->shqd",
            weights.astype(jnp.bfloat16),
            value_part,
            preferred_element_type=jnp.float32,
        )
        return (new_max, new_sum, new_vec)

    def make_fold(query_heads):

        def fold_rows(running, cache_rows, row_start):
            row_span = cache_rows.shape[0]
            per_block = math.gcd(row_span // row_count, max(1, 1024 // row_count))
            block_rows = per_block * row_count

            def block_step(block_index, carried):
                first_row = block_index * block_rows
                cache_block = lax.dynamic_slice_in_dim(cache_rows, first_row, block_rows, 0)
                cache_heads = cache_block.reshape(block_rows, 4, 2, heads_here, HEAD_DIM)
                key_pos = first_row + jnp.arange(block_rows, dtype=jnp.int32)
                plus_part = tuple((member[:2] for member in carried))
                minus_part = tuple((member[2:] for member in carried))
                plus_live = first_row <= my_start + row_count - 1
                minus_live = first_row + block_rows - 1 >= my_start
                plus_next = lax.cond(
                    plus_live,
                    lambda: strand_update(
                        plus_part,
                        query_heads[:2],
                        cache_heads[:, :2, 0],
                        cache_heads[:, :2, 1],
                        key_pos,
                        True,
                    ),
                    lambda: plus_part,
                )
                minus_next = lax.cond(
                    minus_live,
                    lambda: strand_update(
                        minus_part,
                        query_heads[2:],
                        cache_heads[:, 2:, 0],
                        cache_heads[:, 2:, 1],
                        key_pos,
                        False,
                    ),
                    lambda: minus_part,
                )
                return tuple(
                    (
                        jnp.concatenate([plus_item, minus_item], axis=0)
                        for plus_item, minus_item in zip(plus_next, minus_next)
                    )
                )

            return lax.fori_loop(0, row_span // block_rows, block_step, running)

        return fold_rows

    initial = (
        jnp.full((4, heads_here, row_count), NEG_FILL, jnp.float32),
        jnp.zeros((4, heads_here, row_count), jnp.float32),
        jnp.zeros((4, heads_here, row_count, HEAD_DIM), jnp.float32),
    )
    slot_plus = project_all(mutant_rows_plus, query_weight, key_weight, value_weight, slot_plus_pos)
    slot_minus = project_all(
        mutant_rows_minus, query_weight, key_weight, value_weight, slot_minus_pos
    )
    all_queries = jnp.stack(
        [
            ref_plus[0],
            spread(slot_plus[0], ref_plus[0]),
            ref_minus[0],
            spread(slot_minus[0], ref_minus[0]),
        ],
        axis=0,
    ).reshape(4, row_count, heads_here, HEAD_DIM)
    fold_rows = make_fold(all_queries)
    cache_ref = jnp.stack(
        [
            jnp.stack([ref_plus[1], ref_plus[2]], axis=1),
            jnp.stack([ref_minus[1], ref_minus[2]], axis=1),
        ],
        axis=1,
    )
    packet = jnp.stack(
        [
            jnp.stack([slot_plus[1], slot_plus[2]], axis=1),
            jnp.stack([slot_minus[1], slot_minus[2]], axis=1),
        ],
        axis=1,
    )
    shard_start = jnp.int32(0)
    ref_piece = lax.all_gather(cache_ref[None], "ctx", axis=0, tiled=True)
    packet_piece = lax.all_gather(packet[None], "ctx", axis=0, tiled=True)
    shard_count = ref_piece.shape[0]
    row_span = shard_count * row_count
    in_range = (variant_block >= shard_start) & (variant_block < shard_start + shard_count)
    slot_index = variant_block * slot_cap + variant_rank
    slot_hits = (
        (slot_index[:, None] == jnp.arange(shard_count * slot_cap, dtype=jnp.int32)[None, :])
        & in_range[:, None]
    ).astype(jnp.bfloat16)
    row_hits = (
        (variant_sites[:, None] == jnp.arange(row_span, dtype=jnp.int32)[None, :])
        & in_range[:, None]
    ).astype(jnp.bfloat16)
    placing = lax.dot_general(
        row_hits, slot_hits, (((0,), (0,)), ((), ())), preferred_element_type=jnp.float32
    )
    has_key = jnp.sum(placing, axis=1) > 0.5
    flat_packet = packet_piece.reshape(shard_count * slot_cap, 4 * head_width)
    moved = (
        jnp.dot(placing.astype(jnp.bfloat16), flat_packet, preferred_element_type=jnp.float32)
        .astype(jnp.bfloat16)
        .reshape(row_span, 2, 2, head_width)
    )
    flat_ref = ref_piece.reshape(row_span, 2, 2, head_width)
    mutant = jnp.where(has_key[:, None, None, None], moved, flat_ref)
    full_piece = jnp.stack([flat_ref[:, 0], mutant[:, 0], flat_ref[:, 1], mutant[:, 1]], axis=1)
    final = fold_rows(initial, full_piece, shard_start * row_count)
    attended = final[2] / final[1][..., None]
    combined = 0.5 * (attended[0] - attended[1] + (attended[2] - attended[3]))
    combined = combined.transpose(1, 0, 2).reshape(row_count, head_width).astype(jnp.bfloat16)
    summed = lax.psum_scatter(
        lax.dot_general(
            out_weight, combined, (((0,), (1,)), ((), ())), preferred_element_type=jnp.float32
        ).astype(jnp.bfloat16),
        "head",
        scatter_dimension=0,
        tiled=True,
    ).astype(jnp.float32)
    return summed.T.astype(jnp.bfloat16)


def solution(mesh):
    return jax.shard_map(
        shards,
        mesh=mesh,
        in_specs=(
            P(None, ("groups", "ctx"), "head"),
            P(("groups", "ctx")),
            P("groups"),
            P("groups"),
            P(),
            P(None, "head"),
            P(None, "head"),
            P(None, "head"),
            P("head", None),
        ),
        out_specs=P(("groups", "ctx"), "head"),
        check_vma=False,
    )
```

profile of v0, /device:TPU:0, one launch (start us, length us, event | category | flops | bytes accessed | tf_op | source)
XLA Modules:
  0.0 278.4 jit_solution(1111753587806421746)
XLA Ops:
  7.3 6.5 %copy.67 = bf16[512,4096]{1,0:T(8,128)(2,1)} copy(bf16[512,4096]{0,1:T(8,128)(2,1)} %bitcast.148) | data formatting | bytes 8388608 | tf_op jit(solution)/shard_map/dot_general | solution.py:40
  13.8 6.4 %copy.66 = bf16[512,4096]{1,0:T(8,128)(2,1)} copy(bf16[512,4096]{0,1:T(8,128)(2,1)} %bitcast.149) | data formatting | bytes 8388608 | tf_op jit(solution)/shard_map/dot_general | solution.py:40
  23.3 69.1 %all-gather.6.cloned.1.call-done = bf16[2,256,4096]{2,1,0:T(8,128)(2,1)} async-done(((bf16[2,256,1024]{2,1,0:T(8,128)(2,1)}), bf16[2,256,4096]{2,1,0:T(8,128)(2,1)}) %all-gather.6.cloned.1.call-update) | async-done | bytes 4194320 | tf_op jit(solution)/shard_map/all_gather | solution.py:73
  94.6 3.2 %fusion.126 = f32[64,512]{1,0:T(8,128)S(1)} fusion(bf16[64,4096]{1,0:T(8,128)(2,1)S(1)} %fusion.30, bf16[4096,512]{1,0:T(8,128)(2,1)} %param.19), kind=kOutput, calls=%fused_computation.210 | convolution fusion | flops 268435456 | bytes 4849664 | tf_op jit(solution)/shard_map/dot_general | solution.py:40
  106.1 4.3 %fusion.38 = f32[256,4,128]{0,2,1:T(8,128)S(1)} fusion(bf16[4,128,4096]{2,1,0:T(8,128)(2,1)} %bitcast.154, bf16[2,256,4096]{2,1,0:T(8,128)(2,1)} %all-gather.6.cloned.1.call-done), kind=kOutput, calls=%fused_computation.53 | convolution fusion | flops 1073741824 | bytes 6815744 | tf_op jit(solution)/shard_map/dot_general | solution.py:40
  116.9 4.2 %fusion.59 = bf16[256,1,512]{2,0,1:T(8,128)(2,1)S(1)} fusion(bf16[4096,512]{1,0:T(8,128)(2,1)} %param.20, bf16[2,256,4096]{2,1,0:T(8,128)(2,1)} %all-gather.6.cloned.1.call-done), kind=kOutput, calls=%fused_computation.72 | convolution fusion | flops 1073872896 | bytes 6553600 | tf_op jit(solution)/shard_map/dot_general | solution.py:47
  129.4 3.5 %convolution_convert_fusion.1 = bf16[1024,2048]{1,0:T(8,128)(2,1)} fusion(bf16[256,2048]{0,1:T(8,128)(2,1)S(1)} %bitcast.151, bf16[1024,256]{0,1:T(8,128)(2,1)S(1)} %get-tuple-element.230), kind=kOutput, calls=%fused_computation.44 | convolution fusion | flops 1075838976 | bytes 5767168 | tf_op jit(solution)/shard_map/dot_general | solution.py:264
  132.9 6.4 %copy.54 = bf16[1024,2048]{0,1:T(8,128)(2,1)} copy(bf16[1024,2048]{1,0:T(8,128)(2,1)} %convolution_convert_fusion.1) | data formatting | bytes 8388608 | tf_op jit(solution)/shard_map/convert_element_type | solution.py:265
  139.3 6.2 %copy.55 = bf16[1024,2,2,512]{3,0,2,1:T(8,128)(2,1)} copy(bf16[1024,2,2,512]{0,3,2,1:T(8,128)(2,1)} %bitcast.150) | data formatting | bytes 8388608 | tf_op jit(solution)/shard_map/reshape | solution.py:266
  145.5 12.3 %all-gather.8.cloned.1.call-done = bf16[1024,2,2,512]{3,0,2,1:T(8,128)(2,1)} async-done(((bf16[256,2,2,512]{3,0,2,1:T(8,128)(2,1)}), bf16[1024,2,2,512]{3,0,2,1:T(8,128)(2,1)}) %all-gather.8.cloned.1.call-update) | async-done | bytes 4194320 | tf_op jit(solution)/shard_map/all_gather | solution.py:244
  157.8 3.9 %broadcast_select_fusion = bf16[1024,2,2,512]{3,0,2,1:T(8,128)(2,1)S(1)} fusion(bf16[1024,2,2,512]{3,0,2,1:T(8,128)(2,1)} %copy.55, bf16[1024,2,2,512]{3,0,2,1:T(8,128)(2,1)} %all-gather.8.cloned.1.call-done, pred[1024]{0:T(1024)(128)(4,1)S(1)} %broadcast_compare_fusion.2), kind=kLoop, calls=%fused_computation.43 | loop fusion | flops 2097152 | bytes 12583936 | tf_op jit(solution)/shard_map/jit(_where)/select_n | solution.py:269
  164.2 3.9 %pad_maximum_fusion = bf16[1024,4,2,512]{3,0,2,1:T(8,128)(2,1)} fusion(bf16[1024,1,2,512]{3,0,2,1:T(8,128)(2,1)S(1)} %get-tuple-element.187, bf16[1024,1,2,512]{3,0,2,1:T(8,128)(2,1)S(1)} %get-tuple-element.185, bf16[1024,1,2,512]{3,0,2,1:T(8,128)(2,1)S(1)} %get-tuple-element.186, bf16[1024,1,2,512]{3,0,2,1:T(8,128)(2,1)S(1)} %get-tuple-element.184), kind=kLoop, calls=%fused_computation.36 | loop fusion | flops 12582912 | bytes 16777216 | tf_op jit(solution)/shard_map/stack | solution.py:270
  168.1 12.7 %reshape.408 = bf16[1024,4,2,4,128]{4,3,0,2,1:T(4,128)(2,1)} reshape(bf16[1024,4,2,512]{3,0,2,1:T(8,128)(2,1)} %pad_maximum_fusion) | data formatting | bytes 16777216 | tf_op jit(solution)/shard_map/while/body/eval_jaxpr/reshape | solution.py:169
  180.7 21.3 %conditional.3 = (f32[2,4,256]{2,1,0:T(4,128)S(1)}, f32[2,4,256,128]{2,3,1,0:T(8,128)S(1)}) conditional(s32[]{:T(128)} %convert_element_type.229, (f32[2,4,256]{2,1,0:T(4,128)S(1)}, f32[2,4,256,128]{3,2,1,0:T(8,128)S(1)}) %tuple.31, (s32[1024]{0:T(1024)S(1)}, s32[256]{0:T(256)S(1)}, bf16[4,256,4,128]{1,3,2,0:T(8,128)(2,1)S(1)}, ...), branch_computations={%region_12.13_spmd, %region_13.16_spmd} | conditional | flops 1097601024 | bytes 52548624 | solution.py:187
  181.0 8.7 %copy.59 = bf16[1024,4,2,4,128]{4,0,3,1,2:T(8,128)(2,1)} copy(bf16[1024,4,2,4,128]{4,3,0,2,1:T(4,128)(2,1)} %get-tuple-element.160) | data formatting | bytes 16777216 | tf_op jit(solution)/shard_map
  189.6 3.7 %select_reduce_fusion.1 = (f32[2,4,256]{2,1,0:T(4,128)S(1)}, f32[2,4,256,1024]{3,2,1,0:T(8,128)S(1)}) fusion(pred[256,1024]{1,0:T(8,128)(4,1)S(1)} %broadcast_compare_fusion.1, bf16[4,256,4,128]{1,3,2,0:T(8,128)(2,1)S(1)} %get-tuple-element.159, bf16[1024,4,2,4,128]{4,0,3,1,2:T(8,128)(2,1)} %copy.59), kind=kOutput, calls=%fused_computation.19 | convolution fusion | flops 543160320 | bytes 11804672 | tf_op jit(solution)/shard_map/while/body/eval_jaxpr/cond/branch_1_fun/sqhd,kshd->shqk/dot_general | solution.py:139
  193.3 2.6 fusion.15
  195.9 4.6 %fusion.23 = f32[2,4,256,128]{3,2,1,0:T(8,128)} fusion(bf16[1024,4,2,4,128]{4,0,3,1,2:T(8,128)(2,1)} %copy.59, f32[2,4,256,1024]{3,2,1,0:T(8,128)S(1)} %get-tuple-element.183, f32[2,4,256]{2,1,0:T(4,128)S(1)} %max.7, pred[256,1024]{1,0:T(8,128)(4,1)S(1)} %broadcast_compare_fusion.1, f32[2,4,256,128]{3,2,1,0:T(8,128)S(1)} %get-tuple-element.113, ...), kind=kOutput, calls=%fused_computation.30 | convolution fusion | flops 545783808 | bytes 12861440 | tf_op jit(solution)/shard_map/while/body/eval_jaxpr/cond/branch_1_fun/shqk,kshd->shqd/dot_general | solution.py:151
  202.1 21.1 %conditional.2 = (f32[2,4,256]{2,1,0:T(4,128)S(1)}, f32[2,4,256,128]{2,3,1,0:T(8,128)S(1)}) conditional(s32[]{:T(128)} %convert_element_type.199, (f32[2,4,256]{2,1,0:T(4,128)S(1)}, f32[2,4,256,128]{3,2,1,0:T(8,128)S(1)}) %tuple.31, (s32[1024]{0:T(1024)S(1)}, s32[256]{0:T(256)S(1)}, bf16[4,256,4,128]{1,3,2,0:T(8,128)(2,1)S(1)}, ...), branch_computations={%region_8.9_spmd, %region_9.12_spmd} | conditional | flops 1097601024 | bytes 52548624 | solution.py:175
  202.3 8.7 %copy.57 = bf16[1024,4,2,4,128]{4,0,3,1,2:T(8,128)(2,1)} copy(bf16[1024,4,2,4,128]{4,3,0,2,1:T(4,128)(2,1)} %get-tuple-element.153) | data formatting | bytes 16777216 | tf_op jit(solution)/shard_map
  211.0 3.7 %select_reduce_fusion = (f32[2,4,256]{2,1,0:T(4,128)S(1)}, f32[2,4,256,1024]{3,2,1,0:T(8,128)S(1)}) fusion(pred[256,1024]{1,0:T(8,128)(4,1)S(1)} %broadcast_compare_fusion, bf16[4,256,4,128]{1,3,2,0:T(8,128)(2,1)S(1)} %get-tuple-element.152, bf16[1024,4,2,4,128]{4,0,3,1,2:T(8,128)(2,1)} %copy.57), kind=kOutput, calls=%fused_computation.1 | convolution fusion | flops 543160320 | bytes 11804672 | tf_op jit(solution)/shard_map/while/body/eval_jaxpr/cond/branch_1_fun/sqhd,kshd->shqk/dot_general | solution.py:139
  217.0 4.6 %fusion.9 = f32[2,4,256,128]{3,2,1,0:T(8,128)} fusion(bf16[1024,4,2,4,128]{4,0,3,1,2:T(8,128)(2,1)} %copy.57, f32[2,4,256,1024]{3,2,1,0:T(8,128)S(1)} %get-tuple-element.181, f32[2,4,256]{2,1,0:T(4,128)S(1)} %max.6, pred[256,1024]{1,0:T(8,128)(4,1)S(1)} %broadcast_compare_fusion, f32[2,4,256,128]{3,2,1,0:T(8,128)S(1)} %get-tuple-element.106, ...), kind=kOutput, calls=%fused_computation.12 | convolution fusion | flops 545783808 | bytes 12861440 | tf_op jit(solution)/shard_map/while/body/eval_jaxpr/cond/branch_1_fun/shqk,kshd->shqd/dot_general | solution.py:151
  225.4 2.6 fusion.28
  228.0 43.8 %reduce-scatter.2.cloned.1.call-done = bf16[1024,256]{0,1:T(8,128)(2,1)} async-done(((bf16[4096,256]{0,1:T(8,128)(2,1)}), bf16[1024,256]{0,1:T(8,128)(2,1)}) %reduce-scatter.2.cloned.1.call-update) | async-done | bytes 524304 | tf_op jit(solution)/shard_map/reduce_scatter | solution.py:275
  (127 shorter events, 39.1 us)
Async XLA Ops:
  6.5 15.5 %copy-start = (bf16[4,4096]{1,0:T(4,128)(2,1)S(1)}, bf16[4,4096]{1,0:T(4,128)(2,1)}, u32[]{:S(2)}) copy-start(bf16[4,4096]{1,0:T(4,128)(2,1)} %param.17) | copy-start | bytes 98308
  6.5 85.9 %all-gather.6.cloned.1.call-start = ((), (), s32[]{:S(2)}) async-start(), calls=%async_computation.1 | async-start | bytes 5242880 | tf_op jit(solution)/shard_map/all_gather | solution.py:73
  7.3 120.7 %all-gather.10.cloned.1.call-start = ((), (), s32[]{:S(2)}) async-start(), calls=%async_computation.4 | async-start | bytes 1310720 | tf_op jit(solution)/shard_map/all_gather | solution.py:245
  13.8 6.5 %copy-start.15 = (s32[128]{0:T(128)S(1)}, s32[128]{0:T(128)}, u32[]{:S(2)}) copy-start(s32[128]{0:T(128)} %param.15) | copy-start | bytes 1540
  13.8 6.7 %copy-start.14 = (s32[256]{0:T(256)S(1)}, s32[256]{0:T(256)}, u32[]{:S(2)}) copy-start(s32[256]{0:T(256)} %param.14) | copy-start | bytes 3076
  13.8 6.9 %copy-start.16 = (s32[128]{0:T(128)S(1)}, s32[128]{0:T(128)}, u32[]{:S(2)}) copy-start(s32[128]{0:T(128)} %param.16) | copy-start | bytes 1540
  92.4 5.4 %copy-start.3 = (bf16[4096,512]{1,0:T(8,128)(2,1)S(1)}, bf16[4096,512]{1,0:T(8,128)(2,1)}, u32[]{:S(2)}) copy-start(bf16[4096,512]{1,0:T(8,128)(2,1)} %param.18) | copy-start | bytes 12582916
  94.6 4.1 %copy-start.5 = (bf16[4096,512]{1,0:T(8,128)(2,1)S(1)}, bf16[4096,512]{1,0:T(8,128)(2,1)}, u32[]{:S(2)}) copy-start(bf16[4096,512]{1,0:T(8,128)(2,1)} %param.20) | copy-start | bytes 12582916
  97.8 2.3 copy-start.7
  100.1 2.2 copy-start.2
  105.9 51.9 %all-gather.8.cloned.1.call-start = ((), (), s32[]{:S(2)}) async-start(), calls=%async_computation.3 | async-start | bytes 5242880 | tf_op jit(solution)/shard_map/all_gather | solution.py:244
  106.1 4.3 %copy-start.8 = (bf16[2,256,4096]{2,1,0:T(8,128)(2,1)S(1)}, bf16[2,256,4096]{2,1,0:T(8,128)(2,1)}, u32[]{:S(2)}) copy-start(bf16[2,256,4096]{2,1,0:T(8,128)(2,1)} %all-gather.6.cloned.1.call-done) | copy-start | bytes 12582916
  106.1 5.4 %copy-start.11 = (bf16[512,4096]{1,0:T(8,128)(2,1)S(1)}, bf16[512,4096]{1,0:T(8,128)(2,1)}, u32[]{:S(2)}) copy-start(bf16[512,4096]{1,0:T(8,128)(2,1)} %copy.66) | copy-start | bytes 12582916
  111.6 2.3 copy-start.12
  116.9 4.3 %copy-start.6 = (bf16[4096,512]{1,0:T(8,128)(2,1)S(1)}, bf16[4096,512]{1,0:T(8,128)(2,1)}, u32[]{:S(2)}) copy-start(bf16[4096,512]{1,0:T(8,128)(2,1)} %param.20) | copy-start | bytes 12582916
  116.9 5.4 %copy-start.9 = (bf16[2,256,4096]{2,1,0:T(8,128)(2,1)S(1)}, bf16[2,256,4096]{2,1,0:T(8,128)(2,1)}, u32[]{:S(2)}) copy-start(bf16[2,256,4096]{2,1,0:T(8,128)(2,1)} %all-gather.6.cloned.1.call-done) | copy-start | bytes 12582916
  124.7 147.1 %reduce-scatter.2.cloned.1.call-start = ((), (), s32[]{:S(2)}) async-start(), calls=%async_computation.2 | async-start | bytes 2621440 | tf_op jit(solution)/shard_map/reduce_scatter | solution.py:275
  161.7 2.2 copy-start.4
  168.1 12.7 %copy-start.13 = (bf16[4,256,4,128]{1,3,2,0:T(8,128)(2,1)S(1)}, bf16[4,256,4,128]{1,3,2,0:T(8,128)(2,1)}, u32[]{:S(2)}) copy-start(bf16[4,256,4,128]{1,3,2,0:T(8,128)(2,1)} %pad_maximum_fusion.1) | copy-start | bytes 3145732
  223.2 2.2 copy-start.10
  223.6 48.2 %copy-start.1 = (bf16[4,4096]{1,0:T(4,128)(2,1)S(1)}, bf16[4,4096]{1,0:T(4,128)(2,1)}, u32[]{:S(2)}) copy-start(bf16[4,4096]{1,0:T(4,128)(2,1)} %param.17) | copy-start | bytes 98308
Sparse Core Ops, SparseCore 0:
  8.9 83.4 all-gather.5
  106.0 15.1 all-gather.9
  124.9 32.9 all-gather.7
  228.2 43.6 reduce-scatter.1
where the time goes:
time: 280 us; the launch traced here: 278 us
  waiting for transfers between devices  126 us (45%)
  local copies, waits for them, and re-layouts  70.1 us (25%)
  matrix products  48.7 us (17%)
  other arithmetic  19.3 us (7%)
  between operations  13.8 us (5%)
    all_gather x1, waiting for transfers between devices, shards(): gathered = lax.all_gather(hidden, 'head', axis=2, tiled=True)  69.1 us
    reduce_scatter x1, waiting for transfers between devices, shards(): lax.psum_scatter(lax.dot_general(out_weight, combined, (((0,), (1,)), (()...  43.8 us
    another operation x2, local copies, waits for them, and re-layouts  17.4 us
    dot_general x8, matrix products, rotated(): product = jnp.dot(inputs, weight, preferred_element_type=jnp.float32)  13.8 us
    dot_general x2, local copies, waits for them, and re-layouts, rotated(): product = jnp.dot(inputs, weight, preferred_element_type=jnp.float32)  12.9 us
    reshape x1, local copies, waits for them, and re-layouts, block_step(): cache_heads = cache_block.reshape(block_rows, 4, 2, heads_here, HEAD_DIM)  12.7 us
    all_gather x1, waiting for transfers between devices, shards(): ref_piece = lax.all_gather(cache_ref[None], 'ctx', axis=0, tiled=True)  12.3 us
    dot_general x2, matrix products, strand_update(): jnp.einsum('shqk,kshd->shqd', weights.astype(jnp.bfloat16), value_part, p...  9.16 us
  transfers between devices with their start and end apart: 4, of which 3 were waited for; matrix products, arithmetic and copies ran while one was open for 19% of the time, Pallas kernels for 0%

commit v1 on v0

v1 whole, which is shorter than its diff:
```python
import functools
import math

import jax
import jax.numpy as jnp
from jax import lax
from jax.experimental import pallas as pl
from jax.experimental.pallas import tpu as pltpu
from jax.sharding import PartitionSpec as P

HEAD_DIM = 128
VAR_DEV = 32
ROPE_BASE = 10000.0
NEG_FILL = -1e30
FAR = 1 << 29
PIECES = 2
MESH = pl.DeviceIdType.MESH
VMEM_LIMIT = 60 * 1024 * 1024


def greet(axis, size):
    me = lax.axis_index(axis)
    barrier = pltpu.get_barrier_semaphore()

    @pl.when(me > 0)
    def _():
        pl.semaphore_signal(barrier, inc=1, device_id={axis: me - 1}, device_id_type=MESH)

    @pl.when(me < size - 1)
    def _():
        pl.semaphore_signal(barrier, inc=1, device_id={axis: me + 1}, device_id_type=MESH)

    pl.semaphore_wait(barrier, jnp.minimum(me, 1) + jnp.minimum(size - 1 - me, 1))


def project_kernel(
    size,
    hidden,
    wq,
    wk,
    wv,
    sel,
    sel_t,
    has_row,
    codes,
    table,
    cos,
    sin,
    q_out,
    kv_out,
    xbuf,
    wbuf,
    stk,
    acc,
    own_sem,
    w_sem,
    s_sem,
    r_sem,
):
    z = lax.axis_index("head")
    rows, feats = hidden.shape[1], hidden.shape[2]
    slots = sel.shape[0]
    hw = wq.shape[1]
    heads = hw // HEAD_DIM
    piece = rows // PIECES

    greet("head", size)

    def hop(side, strand, shard, part, source):
        span = pl.ds(part * piece, piece)
        return pltpu.make_async_remote_copy(
            src_ref=source.at[strand, span] if source is hidden else xbuf.at[strand, shard, span],
            dst_ref=xbuf.at[strand, shard, span],
            send_sem=s_sem.at[side, strand, shard, part],
            recv_sem=r_sem.at[strand, shard, part],
            device_id={"head": z - 1 if side == 0 else z + 1},
            device_id_type=MESH,
        )

    def send_own(side, strand):
        for part in range(PIECES):
            hop(side, strand, z, part, hidden).start()

    for strand in range(1):

        @pl.when(z > 0)
        def _():
            send_own(0, strand)

        @pl.when(z < size - 1)
        def _():
            send_own(1, strand)

    @pl.when((z > 0) & (z == size - 1))
    def _():
        send_own(0, 1)

    @pl.when((z < size - 1) & (z == 0))
    def _():
        send_own(1, 1)

    own = [
        pltpu.make_async_copy(hidden.at[strand], xbuf.at[strand, z], own_sem.at[strand])
        for strand in range(2)
    ]
    loads = [
        pltpu.make_async_copy(weight, wbuf.at[index], w_sem.at[index])
        for index, weight in enumerate((wq, wk, wv))
    ]
    for copy in own + loads:
        copy.start()
    for copy in own + loads:
        copy.wait()

    shorter = jnp.minimum(z, size - 1 - z)
    long_side = jnp.where(z < size - 1 - z, 1, -1)

    def shard_of(step):
        paired = jnp.where(step % 2 == 1, (step + 1) // 2, -((step + 1) // 2))
        return z + jnp.where(step <= 2 * shorter, paired, long_side * (step - shorter))

    for strand in range(2):
        acc[...] = jnp.zeros_like(acc)

        def step_body(step, carry):
            shard = shard_of(step)
            for part in range(PIECES):

                @pl.when(shard > z)
                def _():
                    hop(0, strand, shard, part, xbuf).wait_recv()

                    @pl.when(z > 0)
                    def _():
                        hop(0, strand, shard, part, xbuf).start()

                @pl.when(shard < z)
                def _():
                    hop(1, strand, shard, part, xbuf).wait_recv()

                    @pl.when(z < size - 1)
                    def _():
                        hop(1, strand, shard, part, xbuf).start()

            if strand == 0:

                @pl.when((shard == size - 1) & (z < size - 1) & (z > 0))
                def _():
                    send_own(0, 1)

                @pl.when((shard == 0) & (z > 0) & (z < size - 1))
                def _():
                    send_own(1, 1)

            block = xbuf[strand, shard]
            stk[pl.ds(0, rows), :] = block
            first = pl.multiple_of(shard * feats, feats)
            diff = jnp.zeros((slots, feats), jnp.float32)
            for code in range(4):
                diff = diff + codes[strand][:, code : code + 1] * table[
                    pl.ds(code, 1), pl.ds(first, feats)
                ]
            picked = jnp.dot(sel[...], block, preferred_element_type=jnp.float32)
            stk[pl.ds(rows, slots), :] = (picked + diff).astype(jnp.bfloat16)
            for index in range(3):
                acc[:, pl.ds(index * hw, hw)] += jnp.dot(
                    stk[...],
                    wbuf[index, pl.ds(first, feats), :],
                    preferred_element_type=jnp.float32,
                )
            return carry

        lax.fori_loop(0, size, step_body, 0)

        cos_part = cos[strand]
        sin_part = sin[strand]
        for head in range(heads):
            cols = pl.ds(head * HEAD_DIM, HEAD_DIM)
            for index in range(2):
                raw = acc[:, pl.ds(index * hw + head * HEAD_DIM, HEAD_DIM)]
                turned = raw * cos_part + pltpu.roll(raw, HEAD_DIM // 2, 1) * sin_part
                turned = turned.astype(jnp.bfloat16)
                if index == 0:
                    base = turned[:rows]
                    placed = jnp.dot(
                        sel_t[...], turned[rows:], preferred_element_type=jnp.float32
                    )
                    q_out[strand, 0, :, cols] = base
                    q_out[strand, 1, :, cols] = jnp.where(
                        has_row[...] > 0.5, placed, base.astype(jnp.float32)
                    ).astype(jnp.bfloat16)
                else:
                    kv_out[strand, :, cols] = turned
        kv_out[strand, :, pl.ds(hw, hw)] = acc[:, pl.ds(2 * hw, hw)].astype(jnp.bfloat16)

    def drain(step, carry):
        shard = shard_of(step)
        for strand in range(2):
            for part in range(PIECES):

                @pl.when((shard >= z) & (z > 0))
                def _():
                    hop(0, strand, shard, part, xbuf).wait_send()

                @pl.when((shard <= z) & (z < size - 1))
                def _():
                    hop(1, strand, shard, part, xbuf).wait_send()

        return carry

    lax.fori_loop(0, size, drain, 0)


def attend_kernel(size, q_in, kv_in, kt_mut, out, kvbuf, m_buf, l_buf, a_buf, s_sem, r_sem):
    me = lax.axis_index("ctx")
    rows, hw = q_in.shape[2], q_in.shape[3]
    heads = hw // HEAD_DIM
    wide = kv_in.shape[1]
    window = rows * size
    log_scale = math.log2(math.e) / math.sqrt(HEAD_DIM)

    greet("ctx", size)

    def hop(strand, shard, own):
        return pltpu.make_async_remote_copy(
            src_ref=kv_in.at[strand] if own else kvbuf.at[strand, shard],
            dst_ref=kvbuf.at[strand, shard],
            send_sem=s_sem.at[strand, shard],
            recv_sem=r_sem.at[strand, shard],
            device_id={"ctx": me + 1 if strand == 0 else me - 1},
            device_id_type=MESH,
        )

    passes_on = (me < size - 1, me > 0)
    for strand in range(2):

        @pl.when(passes_on[strand])
        def _():
            hop(strand, me, True).start()

    row_iota = lax.broadcasted_iota(jnp.int32, (rows, 1), 0)
    col_iota = lax.broadcasted_iota(jnp.int32, (1, rows), 1)

    def clock(strand, block, iota):
        place = block * rows + iota
        return place if strand == 0 else window - 1 - place

    def update(strand, shard, block, first):
        q_time = clock(strand, me, row_iota)
        k_times = (clock(strand, shard, col_iota), kt_mut[strand, shard])
        spans = (rows, wide)

        def one_head(head, carry):
            k_cols = pl.ds(pl.multiple_of(head * HEAD_DIM, HEAD_DIM), HEAD_DIM)
            v_cols = pl.ds(pl.multiple_of(hw + head * HEAD_DIM, HEAD_DIM), HEAD_DIM)
            for kind in range(2):
                span = pl.ds(0, spans[kind])
                raw = lax.dot_general(
                    q_in[strand, kind, :, k_cols],
                    block[span, k_cols],
                    (((1,), (1,)), ((), ())),
                    preferred_element_type=jnp.float32,
                )
                raw = jnp.where(k_times[kind] <= q_time, raw, NEG_FILL)
                top = jnp.max(raw, axis=1, keepdims=True)
                if not first:
                    old = m_buf[strand, head, kind]
                    top = jnp.maximum(old, top)
                    fade = jnp.exp2((old - top) * log_scale)
                weights = jnp.exp2((raw - top) * log_scale)
                total = jnp.sum(weights, axis=1, keepdims=True)
                vec = jnp.dot(
                    weights.astype(jnp.bfloat16),
                    block[span, v_cols],
                    preferred_element_type=jnp.float32,
                )
                if not first:
                    total = total + fade * l_buf[strand, head, kind]
                    vec = vec + fade * a_buf[strand, head, kind]
                m_buf[strand, head, kind] = top
                l_buf[strand, head, kind] = total
                a_buf[strand, head, kind] = vec
            return carry

        lax.fori_loop(0, heads, one_head, 0)

    for strand in range(2):
        update(strand, me, kv_in.at[strand], True)

    def arrive(step, carry):
        shards = (me - step, me + step)
        live = (me - step >= 0, me + step < size)
        for strand in range(2):

            @pl.when(live[strand])
            def _():
                hop(strand, shards[strand], False).wait_recv()

                @pl.when(passes_on[strand])
                def _():
                    hop(strand, shards[strand], False).start()

                update(strand, shards[strand], kvbuf.at[strand, shards[strand]], False)

        return carry

    lax.fori_loop(1, size, arrive, 0)

    for head in range(heads):
        part = [
            a_buf[strand, head, kind] / l_buf[strand, head, kind]
            for strand in range(2)
            for kind in range(2)
        ]
        out[:, pl.ds(head * HEAD_DIM, HEAD_DIM)] = (
            0.5 * ((part[0] - part[1]) + (part[2] - part[3]))
        ).astype(jnp.bfloat16)

    def drain(step, carry):
        shards = (me - step, me + step)
        live = (me - step >= 0, me + step < size)
        for strand in range(2):

            @pl.when(live[strand] & passes_on[strand])
            def _():
                hop(strand, shards[strand], False).wait_send()

        return carry

    lax.fori_loop(0, size, drain, 0)


def vmem():
    return pl.BlockSpec(memory_space=pltpu.VMEM)


def anywhere():
    return pl.BlockSpec(memory_space=pl.ANY)


def shards(
    hidden,
    strand_bases,
    variant_sites,
    base_shift,
    base_embed,
    query_weight,
    key_weight,
    value_weight,
    out_weight,
):
    rows, feats = hidden.shape[1], hidden.shape[2]
    n_head = lax.axis_size("head")
    n_ctx = lax.axis_size("ctx")
    window = rows * n_ctx
    me = lax.axis_index("ctx")
    start = me * rows
    slots = 2 * VAR_DEV
    wide = rows + slots
    hw = query_weight.shape[1]
    heads = hw // HEAD_DIM
    width = query_weight.shape[0]

    count = variant_sites.shape[0]
    order = jnp.arange(count, dtype=jnp.int32)
    row_iota = jnp.arange(rows, dtype=jnp.int32)
    v_block = variant_sites // rows
    before = (v_block[:, None] == v_block[None, :]) & (order[None, :] < order[:, None])
    rank = jnp.sum(before.astype(jnp.int32), axis=1)
    mine = v_block == me
    slot_iota = jnp.arange(slots, dtype=jnp.int32)
    slot_match = (rank[:, None] == slot_iota[None, :]) & mine[:, None]
    row_match = ((variant_sites - start)[:, None] == row_iota[None, :]) & mine[:, None]
    old_base = jnp.sum(jnp.where(row_match, strand_bases[None, :], 0), axis=1)
    new_base = jnp.mod(old_base + base_shift, 4)
    slot_old = jnp.sum(jnp.where(slot_match, old_base[:, None], 0), axis=0)
    slot_new = jnp.sum(jnp.where(slot_match, new_base[:, None], 0), axis=0)
    slot_live = jnp.any(slot_match, axis=0)
    has_row = jnp.any(row_match, axis=0).astype(jnp.float32)[:, None]

    all_slot = v_block * slots + rank
    all_match = all_slot[:, None] == jnp.arange(n_ctx * slots, dtype=jnp.int32)[None, :]
    all_pos = jnp.sum(jnp.where(all_match, variant_sites[:, None], 0), axis=0)
    all_live = jnp.any(all_match, axis=0)
    slot_pos = jnp.sum(jnp.where(slot_match, variant_sites[:, None], 0), axis=0)
    place = jnp.arange(window, dtype=jnp.int32)
    has_key = jnp.any(variant_sites[:, None] == place[None, :], axis=0)
    kt_mut = jnp.stack(
        [
            jnp.concatenate(
                [
                    jnp.where(has_key, FAR, flip(place)).reshape(n_ctx, rows),
                    jnp.where(all_live, flip(all_pos), FAR).reshape(n_ctx, slots),
                ],
                axis=1,
            )
            for flip in (lambda p: p, lambda p: window - 1 - p)
        ]
    )[:, :, None, :]

    sel = (
        (jnp.where(slot_live, slot_pos - start, -1)[:, None] == row_iota[None, :])
    ).astype(jnp.bfloat16)
    sel_t = (
        (row_iota[:, None] == jnp.where(slot_live, slot_pos - start, -1)[None, :])
    ).astype(jnp.bfloat16)
    code_iota = jnp.arange(4, dtype=jnp.int32)

    def signed(new, old):
        hot = (new[:, None] == code_iota[None, :]).astype(jnp.float32) - (
            old[:, None] == code_iota[None, :]
        ).astype(jnp.float32)
        return jnp.where(slot_live[:, None], hot, 0.0)

    codes = jnp.stack([signed(slot_new, slot_old), signed(3 - slot_new, 3 - slot_old)])
    table = base_embed.astype(jnp.float32)

    plus_pos = jnp.concatenate([start + row_iota, slot_pos])
    pos = jnp.stack([plus_pos, window - 1 - plus_pos]).astype(jnp.float32)
    half = HEAD_DIM // 2
    freq = jnp.power(ROPE_BASE, -jnp.arange(half, dtype=jnp.float32) * 2.0 / HEAD_DIM)
    angle = pos[:, :, None] * freq[None, None, :]
    cos_half, sin_half = jnp.cos(angle), jnp.sin(angle)
    cos = jnp.concatenate([cos_half, cos_half], axis=-1)
    sin = jnp.concatenate([-sin_half, sin_half], axis=-1)

    queries, cache = pl.pallas_call(
        functools.partial(project_kernel, n_head),
        out_shape=(
            jax.ShapeDtypeStruct((2, 2, rows, hw), jnp.bfloat16),
            jax.ShapeDtypeStruct((2, wide, 2 * hw), jnp.bfloat16),
        ),
        in_specs=[anywhere()] * 4 + [vmem()] * 7,
        out_specs=(vmem(), vmem()),
        scratch_shapes=[
            pltpu.VMEM((2, n_head, rows, feats), jnp.bfloat16),
            pltpu.VMEM((3, width, hw), jnp.bfloat16),
            pltpu.VMEM((wide, feats), jnp.bfloat16),
            pltpu.VMEM((wide, 3 * hw), jnp.float32),
            pltpu.SemaphoreType.DMA((2,)),
            pltpu.SemaphoreType.DMA((3,)),
            pltpu.SemaphoreType.DMA((2, 2, n_head, PIECES)),
            pltpu.SemaphoreType.DMA((2, n_head, PIECES)),
        ],
        compiler_params=pltpu.CompilerParams(
            collective_id=0, has_side_effects=True, vmem_limit_bytes=VMEM_LIMIT
        ),
        name="project",
    )(
        hidden,
        query_weight,
        key_weight,
        value_weight,
        sel,
        sel_t,
        has_row,
        codes,
        table,
        cos,
        sin,
    )

    combined = pl.pallas_call(
        functools.partial(attend_kernel, n_ctx),
        out_shape=jax.ShapeDtypeStruct((rows, hw), jnp.bfloat16),
        in_specs=[vmem()] * 3,
        out_specs=vmem(),
        scratch_shapes=[
            pltpu.VMEM((2, n_ctx, wide, 2 * hw), jnp.bfloat16),
            pltpu.VMEM((2, heads, 2, rows, 1), jnp.float32),
            pltpu.VMEM((2, heads, 2, rows, 1), jnp.float32),
            pltpu.VMEM((2, heads, 2, rows, HEAD_DIM), jnp.float32),
            pltpu.SemaphoreType.DMA((2, n_ctx)),
            pltpu.SemaphoreType.DMA((2, n_ctx)),
        ],
        compiler_params=pltpu.CompilerParams(
            collective_id=1, has_side_effects=True, vmem_limit_bytes=VMEM_LIMIT
        ),
        name="attend",
    )(queries, cache, kt_mut)

    summed = lax.psum_scatter(
        lax.dot_general(
            out_weight, combined, (((0,), (1,)), ((), ())), preferred_element_type=jnp.float32
        ).astype(jnp.bfloat16),
        "head",
        scatter_dimension=0,
        tiled=True,
    ).astype(jnp.float32)
    return summed.T.astype(jnp.bfloat16)


def solution(mesh):
    return jax.shard_map(
        shards,
        mesh=mesh,
        in_specs=(
            P(None, ("groups", "ctx"), "head"),
            P(("groups", "ctx")),
            P("groups"),
            P("groups"),
            P(),
            P(None, "head"),
            P(None, "head"),
            P(None, "head"),
            P("head", None),
        ),
        out_specs=P(("groups", "ctx"), "head"),
        check_vma=False,
    )
```

time: 280 us -> 186 us (0.66)
  Pallas kernels: 0 us -> 110 us
  waiting for transfers between devices: 126 us -> 44.6 us
  local copies, waits for them, and re-layouts: 70.1 us -> 2.3 us
  matrix products: 48.7 us -> 4.89 us
  other arithmetic: 19.3 us -> 10.9 us
    pallas_call x0 -> x2, Pallas kernels: none -> 110 us  [the longest x1 77.8 us: shards(): pl.pallas_call(functools.partial(project_kernel, n_head), out_shape=(jax....]
    all_gather x3 -> x0, waiting for transfers between devices: 81.4 us -> none  [the longest x1 69.1 us: shards(): gathered = lax.all_gather(hidden, 'head', axis=2, tiled=True)]
    dot_general x25 -> x0, matrix products: 46.1 us -> none  [the longest x8 13.8 us: rotated(): product = jnp.dot(inputs, weight, preferred_element_type=jnp.float32)]
    reshape x6 -> x0, local copies, waits for them, and re-layouts: 19.1 us -> none  [the longest x1 12.7 us: block_step(): cache_heads = cache_block.reshape(block_rows, 4, 2, heads_here, HEAD_DIM)]
    another operation x2, local copies, waits for them, and re-layouts: 17.4 us -> 0.73 us  [the longest x1 0.72 us: shards(): jnp.stack([signed(slot_new, slot_old), signed(3 - slot_new, 3 - slot_old)])]
    dot_general x2 -> x0, local copies, waits for them, and re-layouts: 12.9 us -> none  [rotated(): product = jnp.dot(inputs, weight, preferred_element_type=jnp.float32)]
    unnamed x34 -> x0, local copies, waits for them, and re-layouts: 8.14 us -> none
    another operation x12 -> x3, other arithmetic: 7.68 us -> 0.02 us  [the longest x2 0.01 us: shards(): jnp.stack([jnp.concatenate([jnp.where(has_key, FAR, flip(place)).reshape(...]
  transfers between devices with their start and end apart: 4 -> 1, of which waited for: 3 -> 1; matrix products, arithmetic and copies ran while one was open for 19% -> 0% of each run, Pallas kernels for 0% -> 0%
where the time goes in v1:
time: 186 us
  Pallas kernels  110 us (59%)
  waiting for transfers between devices  44.6 us (24%)
  between operations  13.5 us (7%)
  other arithmetic  10.9 us (6%)
  matrix products  4.89 us (3%)
  local copies, waits for them, and re-layouts  2.3 us (1%)
    pallas_call x1, Pallas kernels, shards(): pl.pallas_call(functools.partial(project_kernel, n_head), out_shape=(jax....  77.8 us
    reduce_scatter x1, waiting for transfers between devices, shards(): lax.psum_scatter(lax.dot_general(out_weight, combined, (((0,), (1,)), (()...  44.5 us
    pallas_call x1, Pallas kernels, shards(): pl.pallas_call(functools.partial(attend_kernel, n_ctx), out_shape=jax.Sha...  32.2 us
    dot_general x1, matrix products, shards(): lax.dot_general(out_weight, combined, (((0,), (1,)), ((), ())), preferred...  4.89 us
  transfers between devices with their start and end apart: 1, of which 1 were waited for; matrix products, arithmetic and copies ran while one was open for 0% of the time, Pallas kernels for 0%

profile of v1, /device:TPU:0, one launch (start us, length us, event | category | flops | bytes accessed | tf_op | source)
XLA Modules:
  0.0 186.1 jit_solution(18107384813995759428)
XLA Ops:
  6.5 0.7 broadcast_compare_fusion
  7.2 0.7 broadcast_subtract_fusion.2
  7.9 0.2 convert_reduce_fusion
  8.1 0.1 fusion.10
  8.2 0.9 select_reduce_fusion.1
  9.0 0.7 and_select_fusion
  9.7 0.8 select_reduce_fusion.3
  10.5 0.7 fusion.3.sel_t
  11.2 0.7 fusion.8.sel
  11.9 0.1 fusion.5
  12.0 0.8 select_reduce_fusion
  12.8 0.1 fusion.2
  12.9 0.8 fusion.1
  13.8 0.7 copy.14.codes
  14.5 0.8 copy.13.has_row
  15.3 1.4 convert_element_type.92.table
  16.7 0.1 reduce_or.45
  16.9 0.6 broadcast_in_dim.128.kt_mut
  17.5 1.2 fusion.6
  18.7 1.1 pad_maximum_fusion
  19.8 77.8 %project.1 = (bf16[2,2,256,512]{3,2,1,0:T(8,128)(2,1)}, bf16[2,320,1024]{2,1,0:T(8,128)(2,1)}) custom-call(bf16[2,256,1024]{2,1,0:T(8,128)(2,1)} %hidden.1, bf16[4096,512]{1,0:T(8,128)(2,1)} %wq.1, bf16[4096,512]{1,0:T(8,128)(2,1)} %wk.1, bf16[4096,512]{1,0:T(8,128)(2,1)} %wv.1, bf16[64,256]{1,0:T(8,128)(2,1)} %fusion.8.sel, bf16[256,64]{1,0:T(8,128)(2,1)} %fusion.3.sel_t, ...), custom_call_target="tpu_custom_call" | custom-call | tf_op jit(solution)/shard_map/project/pallas_call | solution.py:427
  97.6 32.2 %attend.1 = bf16[256,512]{1,0:T(8,128)(2,1)} custom-call(bf16[2,2,256,512]{3,2,1,0:T(8,128)(2,1)} %get-tuple-element.7.q_in, bf16[2,320,1024]{2,1,0:T(8,128)(2,1)} %get-tuple-element.8.kv_in, s32[2,4,1,320]{3,2,1,0:T(1,128)} %broadcast_in_dim.128.kt_mut), custom_call_target="tpu_custom_call" | custom-call | tf_op jit(solution)/shard_map/attend/pallas_call | solution.py:463
  129.8 4.9 %fusion = bf16[4096,256]{0,1:T(8,128)(2,1)} fusion(bf16[256,512]{1,0:T(8,128)(2,1)} %attend.1, bf16[512,4096]{1,0:T(8,128)(2,1)} %param.17), kind=kOutput, calls=%fused_computation.1 | convolution fusion | flops 1074790400 | bytes 6553600 | tf_op jit(solution)/shard_map/dot_general | solution.py:483
  134.7 44.5 %reduce-scatter.2.cloned.1.call-done = bf16[1024,256]{0,1:T(8,128)(2,1)} async-done(((bf16[4096,256]{0,1:T(8,128)(2,1)}), bf16[1024,256]{0,1:T(8,128)(2,1)}) %reduce-scatter.2.cloned.1.call-update) | async-done | bytes 524304 | tf_op jit(solution)/shard_map/reduce_scatter | solution.py:482
  (20 shorter events, 0.2 us)
Async XLA Ops:
  6.5 172.7 %reduce-scatter.2.cloned.1.call-start = ((), (), s32[]{:S(2)}) async-start(), calls=%async_computation.1 | async-start | bytes 2621440 | tf_op jit(solution)/shard_map/reduce_scatter | solution.py:482
Sparse Core Ops, SparseCore 0:
  134.8 44.3 reduce-scatter.1

commit v2 on v1

--- a/solution.py
+++ b/solution.py
@@ -18,19 +18,33 @@
 VMEM_LIMIT = 60 * 1024 * 1024
 
 
-def greet(axis, size):
-    me = lax.axis_index(axis)
+def greet(*axes):
     barrier = pltpu.get_barrier_semaphore()
-
-    @pl.when(me > 0)
-    def _():
-        pl.semaphore_signal(barrier, inc=1, device_id={axis: me - 1}, device_id_type=MESH)
-
-    @pl.when(me < size - 1)
-    def _():
-        pl.semaphore_signal(barrier, inc=1, device_id={axis: me + 1}, device_id_type=MESH)
-
-    pl.semaphore_wait(barrier, jnp.minimum(me, 1) + jnp.minimum(size - 1 - me, 1))
+    peers = 0
+    for axis, size in axes:
+        me = lax.axis_index(axis)
+
+        @pl.when(me > 0)
+        def _():
+            pl.semaphore_signal(barrier, inc=1, device_id={axis: me - 1}, device_id_type=MESH)
+
+        @pl.when(me < size - 1)
+        def _():
+            pl.semaphore_signal(barrier, inc=1, device_id={axis: me + 1}, device_id_type=MESH)
+
+        peers = peers + jnp.minimum(me, 1) + jnp.minimum(size - 1 - me, 1)
+    pl.semaphore_wait(barrier, peers)
+
+
+def near_first(z, size):
+    shorter = jnp.minimum(z, size - 1 - z)
+    long_side = jnp.where(z < size - 1 - z, 1, -1)
+
+    def shard_of(step):
+        paired = jnp.where(step % 2 == 1, (step + 1) // 2, -((step + 1) // 2))
+        return z + jnp.where(step <= 2 * shorter, paired, long_side * (step - shorter))
+
+    return shard_of
 
 
 def project_kernel(
@@ -64,7 +78,7 @@
     heads = hw // HEAD_DIM
     piece = rows // PIECES
 
-    greet("head", size)
+    greet(("head", size))
 
     def hop(side, strand, shard, part, source):
         span = pl.ds(part * piece, piece)
@@ -112,12 +126,7 @@
     for copy in own + loads:
         copy.wait()
 
-    shorter = jnp.minimum(z, size - 1 - z)
-    long_side = jnp.where(z < size - 1 - z, 1, -1)
-
-    def shard_of(step):
-        paired = jnp.where(step % 2 == 1, (step + 1) // 2, -((step + 1) // 2))
-        return z + jnp.where(step <= 2 * shorter, paired, long_side * (step - shorter))
+    shard_of = near_first(z, size)
 
     for strand in range(2):
         acc[...] = jnp.zeros_like(acc)
@@ -211,15 +220,39 @@
     lax.fori_loop(0, size, drain, 0)
 
 
-def attend_kernel(size, q_in, kv_in, kt_mut, out, kvbuf, m_buf, l_buf, a_buf, s_sem, r_sem):
+def attend_kernel(
+    size,
+    n_head,
+    q_in,
+    kv_in,
+    kt_mut,
+    w_in,
+    out,
+    kvbuf,
+    m_buf,
+    l_buf,
+    a_buf,
+    w_buf,
+    gbuf,
+    mine,
+    total_out,
+    s_sem,
+    r_sem,
+    w_sem,
+    gs_sem,
+    gr_sem,
+):
     me = lax.axis_index("ctx")
+    z = lax.axis_index("head")
     rows, hw = q_in.shape[2], q_in.shape[3]
     heads = hw // HEAD_DIM
     wide = kv_in.shape[1]
     window = rows * size
     log_scale = math.log2(math.e) / math.sqrt(HEAD_DIM)
 
-    greet("ctx", size)
+    greet(("ctx", size), ("head", n_head))
+    w_load = pltpu.make_async_copy(w_in, w_buf, w_sem)
+    w_load.start()
 
     def hop(strand, shard, own):
         return pltpu.make_async_remote_copy(
@@ -306,15 +339,83 @@
 
     lax.fori_loop(1, size, arrive, 0)
 
+    def pass_on(side, shard, head, own):
+        return pltpu.make_async_remote_copy(
+            src_ref=mine.at[head] if own else gbuf.at[shard, head],
+            dst_ref=gbuf.at[shard, head],
+            send_sem=gs_sem.at[side, shard, head],
+            recv_sem=gr_sem.at[shard, head],
+            device_id={"head": z - 1 if side == 0 else z + 1},
+            device_id_type=MESH,
+        )
+
     for head in range(heads):
         part = [
             a_buf[strand, head, kind] / l_buf[strand, head, kind]
             for strand in range(2)
             for kind in range(2)
         ]
-        out[:, pl.ds(head * HEAD_DIM, HEAD_DIM)] = (
-            0.5 * ((part[0] - part[1]) + (part[2] - part[3]))
-        ).astype(jnp.bfloat16)
+        mine[head] = (0.5 * ((part[0] - part[1]) + (part[2] - part[3]))).astype(jnp.bfloat16)
+
+        @pl.when(z > 0)
+        def _():
+            pass_on(0, z, head, True).start()
+
+        @pl.when(z < n_head - 1)
+        def _():
+            pass_on(1, z, head, True).start()
+
+    w_load.wait()
+
+    def joined(source):
+        return jnp.concatenate([source[head] for head in range(heads)], axis=1)
+
+    total_out[...] = jnp.dot(joined(mine), w_buf[z], preferred_element_type=jnp.float32)
+    shard_of = near_first(z, n_head)
+
+    def gather_step(step, carry):
+        shard = shard_of(step)
+        for head in range(heads):
+
+            @pl.when(shard > z)
+            def _():
+                pass_on(0, shard, head, False).wait_recv()
+
+                @pl.when(z > 0)
+                def _():
+                    pass_on(0, shard, head, False).start()
+
+            @pl.when(shard < z)
+            def _():
+                pass_on(1, shard, head, False).wait_recv()
+
+                @pl.when(z < n_head - 1)
+                def _():
+                    pass_on(1, shard, head, False).start()
+
+        total_out[...] += jnp.dot(
+            joined(gbuf.at[shard]), w_buf[shard], preferred_element_type=jnp.float32
+        )
+        return carry
+
+    lax.fori_loop(1, n_head, gather_step, 0)
+    out[...] = total_out[...].astype(jnp.bfloat16)
+
+    def drain_gather(step, carry):
+        shard = shard_of(step)
+        for head in range(heads):
+
+            @pl.when((shard >= z) & (z > 0))
+            def _():
+                pass_on(0, shard, head, False).wait_send()
+
+            @pl.when((shard <= z) & (z < n_head - 1))
+            def _():
+                pass_on(1, shard, head, False).wait_send()
+
+        return carry
+
+    lax.fori_loop(0, n_head, drain_gather, 0)
 
     def drain(step, carry):
         shards = (me - step, me + step)
@@ -360,6 +461,26 @@
     hw = query_weight.shape[1]
     heads = hw // HEAD_DIM
     width = query_weight.shape[0]
+
+    z = lax.axis_index("head")
+    n_plane = lax.axis_size("groups") * n_ctx
+    part_rows = hw // n_plane
+    plane = lax.axis_index("groups") * n_ctx + me
+    w_part = lax.dynamic_slice_in_dim(out_weight, plane * part_rows, part_rows, 0)
+
+    def w_block(owner):
+        return lax.dynamic_slice_in_dim(w_part, owner * feats, feats, 1)
+
+    w_mine = jnp.zeros((n_head, part_rows, feats), jnp.bfloat16)
+    for shift in range(n_head):
+        block = w_block(lax.rem(z + shift, n_head))
+        if shift:
+            block = lax.ppermute(
+                block, "head", [(at, (at + shift) % n_head) for at in range(n_head)]
+            )
+        source = lax.rem(z - shift + n_head, n_head)
+        w_mine = lax.dynamic_update_slice(w_mine, block[None], (source, 0, 0))
+    w_all = lax.all_gather(w_mine, ("groups", "ctx"), axis=1, tiled=True)
 
     count = variant_sites.shape[0]
     order = jnp.arange(count, dtype=jnp.int32)
@@ -460,34 +581,31 @@
         sin,
     )
 
-    combined = pl.pallas_call(
-        functools.partial(attend_kernel, n_ctx),
-        out_shape=jax.ShapeDtypeStruct((rows, hw), jnp.bfloat16),
-        in_specs=[vmem()] * 3,
+    return pl.pallas_call(
+        functools.partial(attend_kernel, n_ctx, n_head),
+        out_shape=jax.ShapeDtypeStruct((rows, feats), jnp.bfloat16),
+        in_specs=[vmem()] * 3 + [anywhere()],
         out_specs=vmem(),
         scratch_shapes=[
             pltpu.VMEM((2, n_ctx, wide, 2 * hw), jnp.bfloat16),
             pltpu.VMEM((2, heads, 2, rows, 1), jnp.float32),
             pltpu.VMEM((2, heads, 2, rows, 1), jnp.float32),
             pltpu.VMEM((2, heads, 2, rows, HEAD_DIM), jnp.float32),
+            pltpu.VMEM((n_head, hw, feats), jnp.bfloat16),
+            pltpu.VMEM((n_head, heads, rows, HEAD_DIM), jnp.bfloat16),
+            pltpu.VMEM((heads, rows, HEAD_DIM), jnp.bfloat16),
+            pltpu.VMEM((rows, feats), jnp.float32),
             pltpu.SemaphoreType.DMA((2, n_ctx)),
             pltpu.SemaphoreType.DMA((2, n_ctx)),
+            pltpu.SemaphoreType.DMA(()),
+            pltpu.SemaphoreType.DMA((2, n_head, heads)),
+            pltpu.SemaphoreType.DMA((n_head, heads)),
         ],
         compiler_params=pltpu.CompilerParams(
             collective_id=1, has_side_effects=True, vmem_limit_bytes=VMEM_LIMIT
         ),
         name="attend",
-    )(queries, cache, kt_mut)
-
-    summed = lax.psum_scatter(
-        lax.dot_general(
-            out_weight, combined, (((0,), (1,)), ((), ())), preferred_element_type=jnp.float32
-        ).astype(jnp.bfloat16),
-        "head",
-        scatter_dimension=0,
-        tiled=True,
-    ).astype(jnp.float32)
-    return summed.T.astype(jnp.bfloat16)
+    )(queries, cache, kt_mut, w_all)
 
 
 def solution(mesh):

time: 186 us -> 171 us (0.919)
  waiting for transfers between devices: 44.6 us -> 6.22 us
  Pallas kernels: 110 us -> 125 us
  starting transfers between devices: 0.01 us -> 7.04 us
  local copies, waits for them, and re-layouts: 2.3 us -> 7.41 us
  matrix products: 4.89 us -> 0 us
    reduce_scatter x1 -> x0, waiting for transfers between devices: 44.5 us -> none  [shards(): lax.psum_scatter(lax.dot_general(out_weight, combined, (((0,), (1,)), (()...]
    pallas_call x1, Pallas kernels: 32.2 us -> 48.6 us  [shards(): pl.pallas_call(functools.partial(attend_kernel, n_ctx, n_head), out_shape...]
    ppermute x0 -> x3, starting transfers between devices: none -> 7.04 us  [shards(): lax.ppermute(block, 'head', [(at, (at + shift) % n_head) for at in range(...]
    ppermute x0 -> x3, waiting for transfers between devices: none -> 6.18 us  [shards(): lax.ppermute(block, 'head', [(at, (at + shift) % n_head) for at in range(...]
    dot_general x1 -> x0, matrix products: 4.89 us -> none  [shards(): lax.dot_general(out_weight, combined, (((0,), (1,)), ((), ())), preferred...]
    unnamed x0 -> x3, local copies, waits for them, and re-layouts: none -> 2.66 us
  transfers between devices with their start and end apart: 1 -> 4, of which waited for: 1 -> 2; matrix products, arithmetic and copies ran while one was open for 0% -> 8% of each run, Pallas kernels for 0% -> 45%
where the time goes in v2:
time: 171 us
  Pallas kernels  125 us (73%)
  between operations  13.6 us (8%)
  other arithmetic  10.9 us (6%)
  local copies, waits for them, and re-layouts  7.41 us (4%)
  starting transfers between devices  7.04 us (4%)
  waiting for transfers between devices  6.22 us (4%)
    pallas_call x1, Pallas kernels, shards(): pl.pallas_call(functools.partial(project_kernel, n_head), out_shape=(jax....  76.8 us
    pallas_call x1, Pallas kernels, shards(): pl.pallas_call(functools.partial(attend_kernel, n_ctx, n_head), out_shape...  48.6 us
    ppermute x3, starting transfers between devices, shards(): lax.ppermute(block, 'head', [(at, (at + shift) % n_head) for at in range(...  7.04 us
    ppermute x3, waiting for transfers between devices, shards(): lax.ppermute(block, 'head', [(at, (at + shift) % n_head) for at in range(...  6.18 us
  transfers between devices with their start and end apart: 4, of which 2 were waited for; matrix products, arithmetic and copies ran while one was open for 8% of the time, Pallas kernels for 45%

profile of v2, /device:TPU:0, one launch (start us, length us, event | category | flops | bytes accessed | tf_op | source)
XLA Modules:
  0.0 170.6 jit_solution(3731879919989888675)
XLA Ops:
  6.5 1.3 fusion.12
  7.8 3.1 %collective-permute-start = (bf16[64,1024]{1,0:T(8,128)(2,1)S(1)}, bf16[64,1024]{1,0:T(8,128)(2,1)S(1)}, u32[]{:S(2)}, u32[]{:S(2)}) collective-permute-start(bf16[64,1024]{1,0:T(8,128)(2,1)S(1)} %get-tuple-element.15), channel_id=1, source_target_pairs={{0,1},{1,2},{2,3},{3,0},{4,5},{5,6},{6,7},{7,4},{8,9},{9,10},{10,1... | collective-permute-start | bytes 393224 | tf_op jit(solution)/shard_map/ppermute | solution.py:478
  10.9 2.6 %collective-permute-start.1 = (bf16[64,1024]{1,0:T(8,128)(2,1)S(1)}, bf16[64,1024]{1,0:T(8,128)(2,1)S(1)}, u32[]{:S(2)}, u32[]{:S(2)}) collective-permute-start(bf16[64,1024]{1,0:T(8,128)(2,1)S(1)} %get-tuple-element.16), channel_id=1, source_target_pairs={{0,2},{1,3},{2,0},{3,1},{4,6},{5,7},{6,4},{7,5},{8,10},{9,11},{10,... | collective-permute-start | bytes 393224 | tf_op jit(solution)/shard_map/ppermute | solution.py:478
  13.5 1.3 collective-permute-start.2
  14.9 1.0 bitcast_dynamic-update-slice_fusion.3
  16.0 1.4 collective-permute-done
  17.4 4.7 %collective-permute-done.1 = bf16[64,1024]{1,0:T(8,128)(2,1)S(1)} collective-permute-done((bf16[64,1024]{1,0:T(8,128)(2,1)S(1)}, bf16[64,1024]{1,0:T(8,128)(2,1)S(1)}, u32[]{:S(2)}, u32[]{:S(2)}) %collective-permute-start.1) | collective-permute-done | bytes 131104 | tf_op jit(solution)/shard_map/ppermute | solution.py:478
  22.2 0.8 copy-done
  23.0 0.7 broadcast_subtract_fusion.2
  23.7 0.7 broadcast_compare_fusion
  24.5 0.8 copy.13.has_row
  25.6 0.9 select_reduce_fusion.1
  26.5 0.7 and_select_fusion
  27.1 0.8 select_reduce_fusion.3
  28.0 0.7 copy.14.codes
  28.7 1.4 convert_element_type.81.table
  30.3 0.8 select_reduce_fusion
  31.2 0.8 fusion
  32.7 1.2 fusion.5
  33.9 1.1 pad_maximum_fusion
  35.0 0.7 fusion.7.sel
  36.3 76.8 %project.1 = (bf16[2,2,256,512]{3,2,1,0:T(8,128)(2,1)}, bf16[2,320,1024]{2,1,0:T(8,128)(2,1)}) custom-call(bf16[2,256,1024]{2,1,0:T(8,128)(2,1)} %hidden.1, bf16[4096,512]{1,0:T(8,128)(2,1)} %wq.1, bf16[4096,512]{1,0:T(8,128)(2,1)} %wk.1, bf16[4096,512]{1,0:T(8,128)(2,1)} %wv.1, bf16[64,256]{1,0:T(8,128)(2,1)} %fusion.7.sel, bf16[256,64]{1,0:T(8,128)(2,1)} %fusion.2.sel_t, ...), custom_call_target="tpu_custom_call" | custom-call | tf_op jit(solution)/shard_map/project/pallas_call | solution.py:548
  113.2 48.6 %attend.1 = bf16[256,1024]{1,0:T(8,128)(2,1)} custom-call(bf16[2,2,256,512]{3,2,1,0:T(8,128)(2,1)} %get-tuple-element.7.q_in, bf16[2,320,1024]{2,1,0:T(8,128)(2,1)} %get-tuple-element.8.kv_in, s32[2,4,1,320]{3,2,1,0:T(1,128)} %broadcast_in_dim.143.kt_mut, bf16[4,512,1024]{2,1,0:T(8,128)(2,1)} %all-gather.2.cloned.1.call-done.w_in), custom_call_target="tpu_custom_call" | custom-call | tf_op jit(solution)/shard_map/attend/pallas_call | solution.py:584
  161.8 1.9 %copy.20 = bf16[256,1024]{1,0:T(8,128)(2,1)} copy(bf16[256,1024]{1,0:T(8,128)(2,1)} %attend.1) | data formatting | bytes 1048576
  (34 shorter events, 2.2 us)
Async XLA Ops:
  6.5 106.7 %all-gather.2.cloned.1.call-start = ((), (), s32[]{:S(2)}) async-start(), calls=%async_computation | async-start | bytes 4718592 | tf_op jit(solution)/shard_map/all_gather | solution.py:483
  7.8 9.6 %collective-permute-start = (bf16[64,1024]{1,0:T(8,128)(2,1)S(1)}, bf16[64,1024]{1,0:T(8,128)(2,1)S(1)}, u32[]{:S(2)}, u32[]{:S(2)}) collective-permute-start(bf16[64,1024]{1,0:T(8,128)(2,1)S(1)} %get-tuple-element.15), channel_id=1, source_target_pairs={{0,1},{1,2},{2,3},{3,0},{4,5},{5,6},{6,7},{7,4},{8,9},{9,10},{10,1... | collective-permute-start | bytes 393224 | tf_op jit(solution)/shard_map/ppermute | solution.py:478
  10.9 11.2 %collective-permute-start.1 = (bf16[64,1024]{1,0:T(8,128)(2,1)S(1)}, bf16[64,1024]{1,0:T(8,128)(2,1)S(1)}, u32[]{:S(2)}, u32[]{:S(2)}) collective-permute-start(bf16[64,1024]{1,0:T(8,128)(2,1)S(1)} %get-tuple-element.16), channel_id=1, source_target_pairs={{0,2},{1,3},{2,0},{3,1},{4,6},{5,7},{6,4},{7,5},{8,10},{9,11},{10,... | collective-permute-start | bytes 393224 | tf_op jit(solution)/shard_map/ppermute | solution.py:478
  13.5 8.7 %collective-permute-start.2 = (bf16[64,1024]{1,0:T(8,128)(2,1)S(1)}, bf16[64,1024]{1,0:T(8,128)(2,1)S(1)}, u32[]{:S(2)}, u32[]{:S(2)}) collective-permute-start(bf16[64,1024]{1,0:T(8,128)(2,1)S(1)} %get-tuple-element.14), channel_id=1, source_target_pairs={{0,3},{1,0},{2,1},{3,2},{4,7},{5,4},{6,5},{7,6},{8,11},{9,8},{10,9... | collective-permute-start | bytes 393224 | tf_op jit(solution)/shard_map/ppermute | solution.py:478
  22.2 0.8 copy-start
Sparse Core Ops, SparseCore 0:
  23.2 38.5 all-gather.1

commit v3 on v2

v3 whole, which is shorter than its diff:
```python
import functools
import math

import jax
import jax.numpy as jnp
from jax import lax
from jax.experimental import pallas as pl
from jax.experimental.pallas import tpu as pltpu
from jax.sharding import PartitionSpec as P

HEAD_DIM = 128
VAR_DEV = 32
ROPE_BASE = 10000.0
NEG_FILL = -1e30
FAR = float(1 << 29)
PIECES = 2
MESH = pl.DeviceIdType.MESH
VMEM_LIMIT = 60 * 1024 * 1024


def greet(*axes):
    barrier = pltpu.get_barrier_semaphore()
    peers = 0
    for axis, size in axes:
        me = lax.axis_index(axis)

        @pl.when(me > 0)
        def _():
            pl.semaphore_signal(barrier, inc=1, device_id={axis: me - 1}, device_id_type=MESH)

        @pl.when(me < size - 1)
        def _():
            pl.semaphore_signal(barrier, inc=1, device_id={axis: me + 1}, device_id_type=MESH)

        peers = peers + jnp.minimum(me, 1) + jnp.minimum(size - 1 - me, 1)
    pl.semaphore_wait(barrier, peers)


def greet_all(axis, size):
    me = lax.axis_index(axis)
    barrier = pltpu.get_barrier_semaphore()
    for shift in range(1, size):
        pl.semaphore_signal(
            barrier, inc=1, device_id={axis: (me + shift) % size}, device_id_type=MESH
        )
    pl.semaphore_wait(barrier, size - 1)


def iota(shape, axis):
    return lax.broadcasted_iota(jnp.int32, shape, axis).astype(jnp.float32)


def to_column(row):
    size = row.shape[1]
    eye = iota((size, 1), 0) == iota((1, size), 1)
    return jnp.sum(jnp.where(eye, row, 0.0), axis=1, keepdims=True)


def slot_of(sites_row, sites_col, begin, rows):
    count = sites_row.shape[1]

    def inside(sites):
        return jnp.where((sites >= begin) & (sites < begin + rows), 1.0, 0.0)

    in_row, in_col = inside(sites_row), inside(sites_col)
    at_row, at_col = iota((1, count), 1), iota((count, 1), 0)
    rank_col = jnp.sum(jnp.where(at_row < at_col, in_row, 0.0), axis=1, keepdims=True)
    rank_row = jnp.sum(jnp.where(at_col < at_row, in_col, 0.0), axis=0, keepdims=True)
    return (
        jnp.where(in_row > 0.5, rank_row, -1.0),
        jnp.where(in_col > 0.5, rank_col, -1.0),
    )


def slot_row(slot_col, sites_col, slots):
    match = slot_col == iota((1, slots), 1)
    place = jnp.sum(jnp.where(match, sites_col, 0.0), axis=0, keepdims=True)
    live = jnp.sum(jnp.where(match, 1.0, 0.0), axis=0, keepdims=True)
    return place, live


def near_first(z, size):
    shorter = jnp.minimum(z, size - 1 - z)
    long_side = jnp.where(z < size - 1 - z, 1, -1)

    def shard_of(step):
        paired = jnp.where(step % 2 == 1, (step + 1) // 2, -((step + 1) // 2))
        return z + jnp.where(step <= 2 * shorter, paired, long_side * (step - shorter))

    return shard_of


class Layer:
    def __init__(self, size, slots, strand, hidden, weights, small, work, sems):
        self.size, self.slots, self.strand = size, slots, strand
        self.hidden, self.weights = hidden, weights
        self.sites, self.shift, self.bases, self.embed, self.freq = small
        self.xbuf, self.wbuf, self.stk, self.acc = work
        self.own_sem, self.w_sem, self.s_sem, self.r_sem = sems
        self.z = lax.axis_index("head")
        self.rows, self.feats = hidden.shape[1], hidden.shape[2]
        self.hw = weights[0].shape[1]
        self.piece = self.rows // PIECES
        self.shard_of = near_first(self.z, size)

    def hop(self, side, shard, part, own=False):
        span = pl.ds(part * self.piece, self.piece)
        return pltpu.make_async_remote_copy(
            src_ref=self.hidden.at[self.strand, span] if own else self.xbuf.at[shard, span],
            dst_ref=self.xbuf.at[shard, span],
            send_sem=self.s_sem.at[side, shard, part],
            recv_sem=self.r_sem.at[shard, part],
            device_id={"head": self.z - 1 if side == 0 else self.z + 1},
            device_id_type=MESH,
        )

    def open(self):
        z = self.z
        for part in range(PIECES):

            @pl.when(z > 0)
            def _():
                self.hop(0, z, part, True).start()

            @pl.when(z < self.size - 1)
            def _():
                self.hop(1, z, part, True).start()

    def load(self):
        copies = [
            pltpu.make_async_copy(
                self.hidden.at[self.strand], self.xbuf.at[self.z], self.own_sem
            )
        ] + [
            pltpu.make_async_copy(weight, self.wbuf.at[index], self.w_sem.at[index])
            for index, weight in enumerate(self.weights)
        ]
        for copy in copies:
            copy.start()
        return copies

    def tables(self):
        rows, slots = self.rows, self.slots
        me = lax.axis_index("ctx")
        begin = (me * rows).astype(jnp.float32)
        window = rows * lax.axis_size("ctx")
        sites_row = self.sites[...].astype(jnp.float32)
        sites_col = to_column(sites_row)
        slot_r, slot_c = slot_of(sites_row, sites_col, begin, rows)
        place_r, live_r = slot_row(slot_c, sites_col, slots)
        match_t = iota((slots, 1), 0) == slot_r
        place_c = jnp.sum(jnp.where(match_t, sites_row, 0.0), axis=1, keepdims=True)
        self.live = jnp.sum(jnp.where(match_t, 1.0, 0.0), axis=1, keepdims=True)
        shift = jnp.sum(
            jnp.where(match_t, self.shift[...].astype(jnp.float32), 0.0), axis=1, keepdims=True
        )
        local_c = jnp.where(self.live > 0.5, place_c - begin, -1.0)
        local_r = jnp.where(live_r > 0.5, place_r - begin, -1.0)
        hit = local_c == iota((1, rows), 1)
        hit_t = iota((rows, 1), 0) == local_r
        self.sel = jnp.where(hit, 1.0, 0.0).astype(jnp.bfloat16)
        spread = jnp.where(hit_t, 1.0, 0.0)
        self.sel_t = spread.astype(jnp.bfloat16)
        self.has_row = jnp.sum(spread, axis=1, keepdims=True)
        old = jnp.sum(
            jnp.where(hit, self.bases[...].astype(jnp.float32), 0.0), axis=1, keepdims=True
        )
        new = old + shift
        new = jnp.where(new >= 4.0, new - 4.0, new)
        if self.strand == 1:
            old, new = 3.0 - old, 3.0 - new
        self.coefs = [
            jnp.where(
                self.live > 0.5,
                jnp.where(new == code, 1.0, 0.0) - jnp.where(old == code, 1.0, 0.0),
                0.0,
            )
            for code in range(4)
        ]
        place = jnp.concatenate([begin + iota((rows, 1), 0), place_c], axis=0)
        if self.strand == 1:
            place = window - 1 - place
        angle = place * self.freq[...]
        self.cos = jnp.cos(angle)
        side = jnp.where(iota((1, HEAD_DIM), 1) < HEAD_DIM // 2, -1.0, 1.0)
        self.sin = jnp.sin(angle) * side

    def run(self, between=None):
        z, size, rows, feats, hw = self.z, self.size, self.rows, self.feats, self.hw
        self.acc[...] = jnp.zeros_like(self.acc)

        def step_body(step, carry):
            shard = self.shard_of(step)
            for part in range(PIECES):

                @pl.when(shard > z)
                def _():
                    self.hop(0, shard, part).wait_recv()

                    @pl.when(z > 0)
                    def _():
                        self.hop(0, shard, part).start()

                @pl.when(shard < z)
                def _():
                    self.hop(1, shard, part).wait_recv()

                    @pl.when(z < size - 1)
                    def _():
                        self.hop(1, shard, part).start()

            block = self.xbuf[shard]
            self.stk[pl.ds(0, rows), :] = block
            first = pl.multiple_of(shard * feats, feats)
            letters = self.embed[:, pl.ds(first, feats)].astype(jnp.float32)
            diff = sum(self.coefs[code] * letters[code : code + 1] for code in range(4))
            picked = jnp.dot(self.sel, block, preferred_element_type=jnp.float32)
            self.stk[pl.ds(rows, self.slots), :] = (picked + diff).astype(jnp.bfloat16)
            for index in range(3):
                self.acc[:, pl.ds(index * hw, hw)] += jnp.dot(
                    self.stk[...],
                    self.wbuf[index, pl.ds(first, feats), :],
                    preferred_element_type=jnp.float32,
                )
            if between is not None:
                between(step)
            return carry

        lax.fori_loop(0, size, step_body, 0)

    def finish(self, q_out, kv_out):
        rows, hw = self.rows, self.hw
        for head in range(hw // HEAD_DIM):
            cols = pl.ds(head * HEAD_DIM, HEAD_DIM)
            for index in range(2):
                raw = self.acc[:, pl.ds(index * hw + head * HEAD_DIM, HEAD_DIM)]
                turned = raw * self.cos + pltpu.roll(raw, HEAD_DIM // 2, 1) * self.sin
                turned = turned.astype(jnp.bfloat16)
                if index == 0:
                    base = turned[:rows]
                    placed = jnp.dot(
                        self.sel_t, turned[rows:], preferred_element_type=jnp.float32
                    )
                    q_out[0, :, cols] = base
                    q_out[1, :, cols] = jnp.where(
                        self.has_row > 0.5, placed, base.astype(jnp.float32)
                    ).astype(jnp.bfloat16)
                else:
                    kv_out[:, cols] = turned
        kv_out[:, pl.ds(hw, hw)] = self.acc[:, pl.ds(2 * hw, hw)].astype(jnp.bfloat16)

    def drain(self):
        z = self.z

        def body(step, carry):
            shard = self.shard_of(step)
            for part in range(PIECES):

                @pl.when((shard >= z) & (z > 0))
                def _():
                    self.hop(0, shard, part).wait_send()

                @pl.when((shard <= z) & (z < self.size - 1))
                def _():
                    self.hop(1, shard, part).wait_send()

            return carry

        lax.fori_loop(0, self.size, body, 0)


class Attention:
    def __init__(self, size, slots, strand, q_in, kv_in, sites, work):
        self.size, self.slots, self.strand = size, slots, strand
        self.q_in, self.kv_in = q_in, kv_in
        self.kvbuf, self.m_buf, self.l_buf, self.a_buf, self.s_sem, self.r_sem = work
        self.me = lax.axis_index("ctx")
        self.rows, self.hw = q_in.shape[1], q_in.shape[2]
        self.heads = self.hw // HEAD_DIM
        self.window = self.rows * size
        self.passes_on = self.me < size - 1 if strand == 0 else self.me > 0
        self.sites_row = sites[...].astype(jnp.float32)
        self.sites_col = to_column(self.sites_row)

    def hop(self, shard, own=False):
        return pltpu.make_async_remote_copy(
            src_ref=self.kv_in if own else self.kvbuf.at[shard],
            dst_ref=self.kvbuf.at[shard],
            send_sem=self.s_sem.at[shard],
            recv_sem=self.r_sem.at[shard],
            device_id={"ctx": self.me + 1 if self.strand == 0 else self.me - 1},
            device_id_type=MESH,
        )

    def open(self):
        @pl.when(self.passes_on)
        def _():
            self.hop(self.me, True).start()

    def clock(self, place):
        return place if self.strand == 0 else self.window - 1 - place

    def update(self, shard, block, first):
        rows, hw, slots = self.rows, self.hw, self.slots
        q_time = self.clock((self.me * rows).astype(jnp.float32) + iota((rows, 1), 0))
        begin = (shard * rows).astype(jnp.float32)
        place = begin + iota((1, rows), 1)
        ref_time = self.clock(place)
        _, slot_c = slot_of(self.sites_row, self.sites_col, begin, rows)
        slot_place, live = slot_row(slot_c, self.sites_col, slots)
        taken = jnp.sum(jnp.where(self.sites_col == place, 1.0, 0.0), axis=0, keepdims=True)
        mut_time = jnp.concatenate(
            [
                jnp.where(taken > 0.5, FAR, ref_time),
                jnp.where(live > 0.5, self.clock(slot_place), FAR),
            ],
            axis=1,
        )
        k_times = (ref_time, mut_time)
        spans = (rows, rows + slots)
        log_scale = math.log2(math.e) / math.sqrt(HEAD_DIM)

        def one_head(head, carry):
            k_cols = pl.ds(pl.multiple_of(head * HEAD_DIM, HEAD_DIM), HEAD_DIM)
            v_cols = pl.ds(pl.multiple_of(hw + head * HEAD_DIM, HEAD_DIM), HEAD_DIM)
            for kind in range(2):
                span = pl.ds(0, spans[kind])
                raw = lax.dot_general(
                    self.q_in[kind, :, k_cols],
                    block[span, k_cols],
                    (((1,), (1,)), ((), ())),
                    preferred_element_type=jnp.float32,
                )
                raw = jnp.where(k_times[kind] <= q_time, raw, NEG_FILL)
                top = jnp.max(raw, axis=1, keepdims=True)
                if not first:
                    old = self.m_buf[head, kind]
                    top = jnp.maximum(old, top)
                    fade = jnp.exp2((old - top) * log_scale)
                weights = jnp.exp2((raw - top) * log_scale)
                total = jnp.sum(weights, axis=1, keepdims=True)
                vec = jnp.dot(
                    weights.astype(jnp.bfloat16),
                    block[span, v_cols],
                    preferred_element_type=jnp.float32,
                )
                if not first:
                    total = total + fade * self.l_buf[head, kind]
                    vec = vec + fade * self.a_buf[head, kind]
                self.m_buf[head, kind] = top
                self.l_buf[head, kind] = total
                self.a_buf[head, kind] = vec
            return carry

        lax.fori_loop(0, self.heads, one_head, 0)

    def own_block(self):
        self.update(self.me, self.kv_in, True)

    def shard_at(self, step):
        return self.me - step if self.strand == 0 else self.me + step

    def alive(self, step):
        shard = self.shard_at(step)
        return shard >= 0 if self.strand == 0 else shard < self.size

    def arrive(self, step):
        shard = self.shard_at(step)

        @pl.when(self.alive(step))
        def _():
            self.hop(shard).wait_recv()

            @pl.when(self.passes_on)
            def _():
                self.hop(shard).start()

            self.update(shard, self.kvbuf.at[shard], False)

    def change(self, head):
        return self.a_buf[head, 0] / self.l_buf[head, 0] - self.a_buf[head, 1] / self.l_buf[head, 1]

    def drain(self):
        def body(step, carry):
            @pl.when(self.alive(step) & self.passes_on)
            def _():
                self.hop(self.shard_at(step)).wait_send()

            return carry

        lax.fori_loop(0, self.size, body, 0)


def plus_kernel(
    n_head,
    slots,
    hidden,
    wq,
    wk,
    wv,
    out_w,
    sites,
    shift,
    bases,
    embed,
    freq,
    q_out,
    kv_out,
    w_out,
    *rest,
):
    work, sems, (x_send, x_recv, x_own) = rest[:4], rest[4:8], rest[8:]
    z = lax.axis_index("head")
    plane = lax.axis_index("groups") * lax.axis_size("ctx") + lax.axis_index("ctx")
    part, feats = w_out.shape[1], w_out.shape[2]
    part_rows = pl.ds(pl.multiple_of(plane * part, part), part)
    greet_all("head", n_head)
    layer = Layer(
        n_head, slots, 0, hidden, (wq, wk, wv), (sites, shift, bases, embed, freq), work, sems
    )
    layer.open()

    def trade(shift):
        owner = (z + shift) % n_head
        cols = pl.ds(pl.multiple_of(owner * feats, feats), feats)
        return pltpu.make_async_remote_copy(
            src_ref=out_w.at[part_rows, cols],
            dst_ref=w_out.at[z],
            send_sem=x_send.at[owner],
            recv_sem=x_recv.at[z],
            device_id={"head": owner},
            device_id_type=MESH,
        )

    def traded(shift):
        source = (z + shift) % n_head
        cols = pl.ds(pl.multiple_of(z * feats, feats), feats)
        return pltpu.make_async_remote_copy(
            src_ref=out_w.at[part_rows, cols],
            dst_ref=w_out.at[source],
            send_sem=x_send.at[source],
            recv_sem=x_recv.at[source],
            device_id={"head": source},
            device_id_type=MESH,
        )

    for step in range(1, n_head):
        trade(step).start()
    keep = pltpu.make_async_copy(
        out_w.at[part_rows, pl.ds(pl.multiple_of(z * feats, feats), feats)], w_out.at[z], x_own
    )
    loads = layer.load() + [keep]
    keep.start()
    layer.tables()
    for copy in loads:
        copy.wait()
    layer.run()
    layer.finish(q_out, kv_out)
    for step in range(1, n_head):
        traded(step).wait_recv()
        trade(step).wait_send()
    layer.drain()


def minus_kernel(
    n_head,
    n_ctx,
    slots,
    hidden,
    wq,
    wk,
    wv,
    sites,
    shift,
    bases,
    embed,
    freq,
    q_plus,
    kv_plus,
    q_out,
    kv_out,
    change,
    *rest,
):
    work, sems, seen = rest[:4], rest[4:8], rest[8:]
    greet(("head", n_head), ("ctx", n_ctx))
    layer = Layer(
        n_head, slots, 1, hidden, (wq, wk, wv), (sites, shift, bases, embed, freq), work, sems
    )
    attention = Attention(n_ctx, slots, 0, q_plus, kv_plus, sites, seen)
    layer.open()
    attention.open()
    loads = layer.load()
    layer.tables()
    attention.own_block()
    for copy in loads:
        copy.wait()

    def between(step):
        span = max(n_head - 2, 1)
        low = 1 + jnp.maximum(step - 1, 0) * (n_ctx - 1) // span
        high = 1 + step * (n_ctx - 1) // span
        high = jnp.minimum(high, n_ctx)

        def body(at, carry):
            attention.arrive(at)
            return carry

        lax.fori_loop(low, high, body, 0)

    layer.run(between)
    layer.finish(q_out, kv_out)
    for head in range(attention.heads):
        change[head] = attention.change(head)
    attention.drain()
    layer.drain()


def last_kernel(
    n_head,
    n_ctx,
    slots,
    q_in,
    kv_in,
    sites,
    change,
    w_in,
    out,
    w_buf,
    gbuf,
    mine,
    total_out,
    w_sem,
    gs_sem,
    gr_sem,
    *seen,
):
    z = lax.axis_index("head")
    greet(("ctx", n_ctx), ("head", n_head))
    attention = Attention(n_ctx, slots, 1, q_in, kv_in, sites, seen)
    heads = attention.heads
    attention.open()
    w_load = pltpu.make_async_copy(w_in, w_buf, w_sem)
    w_load.start()
    attention.own_block()

    def body(at, carry):
        attention.arrive(at)
        return carry

    lax.fori_loop(1, n_ctx, body, 0)

    def pass_on(side, shard, head, own):
        return pltpu.make_async_remote_copy(
            src_ref=mine.at[head] if own else gbuf.at[shard, head],
            dst_ref=gbuf.at[shard, head],
            send_sem=gs_sem.at[side, shard, head],
            recv_sem=gr_sem.at[shard, head],
            device_id={"head": z - 1 if side == 0 else z + 1},
            device_id_type=MESH,
        )

    for head in range(heads):
        mine[head] = (0.5 * (change[head] + attention.change(head))).astype(jnp.bfloat16)

        @pl.when(z > 0)
        def _():
            pass_on(0, z, head, True).start()

        @pl.when(z < n_head - 1)
        def _():
            pass_on(1, z, head, True).start()

    w_load.wait()

    def joined(source):
        return jnp.concatenate([source[head] for head in range(heads)], axis=1)

    total_out[...] = jnp.dot(joined(mine), w_buf[z], preferred_element_type=jnp.float32)
    shard_of = near_first(z, n_head)

    def gather_step(step, carry):
        shard = shard_of(step)
        for head in range(heads):

            @pl.when(shard > z)
            def _():
                pass_on(0, shard, head, False).wait_recv()

                @pl.when(z > 0)
                def _():
                    pass_on(0, shard, head, False).start()

            @pl.when(shard < z)
            def _():
                pass_on(1, shard, head, False).wait_recv()

                @pl.when(z < n_head - 1)
                def _():
                    pass_on(1, shard, head, False).start()

        total_out[...] += jnp.dot(
            joined(gbuf.at[shard]), w_buf[shard], preferred_element_type=jnp.float32
        )
        return carry

    lax.fori_loop(1, n_head, gather_step, 0)
    out[...] = total_out[...].astype(jnp.bfloat16)

    def drain_gather(step, carry):
        shard = shard_of(step)
        for head in range(heads):

            @pl.when((shard >= z) & (z > 0))
            def _():
                pass_on(0, shard, head, False).wait_send()

            @pl.when((shard <= z) & (z < n_head - 1))
            def _():
                pass_on(1, shard, head, False).wait_send()

        return carry

    lax.fori_loop(0, n_head, drain_gather, 0)
    attention.drain()


def vmem():
    return pl.BlockSpec(memory_space=pltpu.VMEM)


def anywhere():
    return pl.BlockSpec(memory_space=pl.ANY)


def shards(
    hidden,
    strand_bases,
    variant_sites,
    base_shift,
    base_embed,
    query_weight,
    key_weight,
    value_weight,
    out_weight,
):
    rows, feats = hidden.shape[1], hidden.shape[2]
    n_head = lax.axis_size("head")
    n_ctx = lax.axis_size("ctx")
    slots = 2 * VAR_DEV
    wide = rows + slots
    width, hw = query_weight.shape
    heads = hw // HEAD_DIM
    part = hw // (lax.axis_size("groups") * n_ctx)

    half = HEAD_DIM // 2
    freq = jnp.power(ROPE_BASE, -jnp.arange(half, dtype=jnp.float32) * 2.0 / HEAD_DIM)
    small = (
        variant_sites[None, :],
        base_shift[None, :],
        strand_bases[None, :],
        base_embed,
        jnp.concatenate([freq, freq])[None, :],
    )
    weights = (query_weight, key_weight, value_weight)
    layer_work = [
        pltpu.VMEM((n_head, rows, feats), jnp.bfloat16),
        pltpu.VMEM((3, width, hw), jnp.bfloat16),
        pltpu.VMEM((wide, feats), jnp.bfloat16),
        pltpu.VMEM((wide, 3 * hw), jnp.float32),
        pltpu.SemaphoreType.DMA(()),
        pltpu.SemaphoreType.DMA((3,)),
        pltpu.SemaphoreType.DMA((2, n_head, PIECES)),
        pltpu.SemaphoreType.DMA((n_head, PIECES)),
    ]
    attend_work = [
        pltpu.VMEM((n_ctx, wide, 2 * hw), jnp.bfloat16),
        pltpu.VMEM((heads, 2, rows, 1), jnp.float32),
        pltpu.VMEM((heads, 2, rows, 1), jnp.float32),
        pltpu.VMEM((heads, 2, rows, HEAD_DIM), jnp.float32),
        pltpu.SemaphoreType.DMA((n_ctx,)),
        pltpu.SemaphoreType.DMA((n_ctx,)),
    ]
    q_shape = jax.ShapeDtypeStruct((2, rows, hw), jnp.bfloat16)
    kv_shape = jax.ShapeDtypeStruct((wide, 2 * hw), jnp.bfloat16)

    def call(kernel, number, out_shape, in_specs, scratch, name):
        return pl.pallas_call(
            kernel,
            out_shape=out_shape,
            in_specs=in_specs,
            out_specs=jax.tree.map(lambda _: vmem(), out_shape),
            scratch_shapes=scratch,
            compiler_params=pltpu.CompilerParams(
                collective_id=number, has_side_effects=True, vmem_limit_bytes=VMEM_LIMIT
            ),
            name=name,
        )

    q_plus, kv_plus, w_mine = call(
        functools.partial(plus_kernel, n_head, slots),
        0,
        (q_shape, kv_shape, jax.ShapeDtypeStruct((n_head, part, feats), jnp.bfloat16)),
        [anywhere()] * 5 + [vmem()] * 5,
        layer_work
        + [
            pltpu.SemaphoreType.DMA((n_head,)),
            pltpu.SemaphoreType.DMA((n_head,)),
            pltpu.SemaphoreType.DMA(()),
        ],
        "project_plus",
    )(hidden, *weights, out_weight, *small)
    w_all = lax.all_gather(w_mine, ("groups", "ctx"), axis=1, tiled=True)
    q_minus, kv_minus, change = call(
        functools.partial(minus_kernel, n_head, n_ctx, slots),
        1,
        (q_shape, kv_shape, jax.ShapeDtypeStruct((heads, rows, HEAD_DIM), jnp.float32)),
        [anywhere()] * 4 + [vmem()] * 7,
        layer_work + attend_work,
        "attend_plus",
    )(hidden, *weights, *small, q_plus, kv_plus)
    return call(
        functools.partial(last_kernel, n_head, n_ctx, slots),
        2,
        jax.ShapeDtypeStruct((rows, feats), jnp.bfloat16),
        [vmem()] * 4 + [anywhere()],
        [
            pltpu.VMEM((n_head, hw, feats), jnp.bfloat16),
            pltpu.VMEM((n_head, heads, rows, HEAD_DIM), jnp.bfloat16),
            pltpu.VMEM((heads, rows, HEAD_DIM), jnp.bfloat16),
            pltpu.VMEM((rows, feats), jnp.float32),
            pltpu.SemaphoreType.DMA(()),
            pltpu.SemaphoreType.DMA((2, n_head, heads)),
            pltpu.SemaphoreType.DMA((n_head, heads)),
        ]
        + attend_work,
        "attend_minus",
    )(q_minus, kv_minus, small[0], change, w_all)


def solution(mesh):
    return jax.shard_map(
        shards,
        mesh=mesh,
        in_specs=(
            P(None, ("groups", "ctx"), "head"),
            P(("groups", "ctx")),
            P("groups"),
            P("groups"),
            P(),
            P(None, "head"),
            P(None, "head"),
            P(None, "head"),
            P("head", None),
        ),
        out_specs=P(("groups", "ctx"), "head"),
        check_vma=False,
    )
```

time: 171 us -> 159 us (0.930)
  Pallas kernels: 125 us -> 142 us
  other arithmetic: 10.9 us -> 0.6 us
  starting transfers between devices: 7.04 us -> 0.01 us
  waiting for transfers between devices: 6.22 us -> 0.04 us
  local copies, waits for them, and re-layouts: 7.41 us -> 1.87 us
    pallas_call x2 -> x3, Pallas kernels: 125 us -> 142 us  [the longest x1 52.5 us: shards(): call(functools.partial(plus_kernel, n_head, slots), 0, (q_shape, kv_shape...]
    ppermute x3 -> x0, starting transfers between devices: 7.04 us -> none  [shards(): lax.ppermute(block, 'head', [(at, (at + shift) % n_head) for at in range(...]
    ppermute x3 -> x0, waiting for transfers between devices: 6.18 us -> none  [shards(): lax.ppermute(block, 'head', [(at, (at + shift) % n_head) for at in range(...]
    convert_element_type x5 -> x0, other arithmetic: 2.72 us -> none  [the longest x1 1.38 us: shards(): table = base_embed.astype(jnp.float32)]
    reduce_sum x4 -> x0, other arithmetic: 2.62 us -> none  [the longest x1 0.88 us: shards(): old_base = jnp.sum(jnp.where(row_match, strand_bases[None, :], 0), axis=1)]
  transfers between devices with their start and end apart: 4 -> 1, of which waited for: 2 -> 0; matrix products, arithmetic and copies ran while one was open for 8% -> 0% of each run, Pallas kernels for 45% -> 26%
where the time goes in v3:
time: 159 us; the launch traced here: 158 us
  Pallas kernels  142 us (89%)
  between operations  13.4 us (8%)
  local copies, waits for them, and re-layouts  1.87 us (1%)
    pallas_call x1, Pallas kernels, shards(): call(functools.partial(plus_kernel, n_head, slots), 0, (q_shape, kv_shape...  52.5 us
    pallas_call x1, Pallas kernels, shards(): call(functools.partial(last_kernel, n_head, n_ctx, slots), 2, jax.ShapeDt...  49.4 us
    pallas_call x1, Pallas kernels, shards(): call(functools.partial(minus_kernel, n_head, n_ctx, slots), 1, (q_shape,...  40.5 us
  transfers between devices with their start and end apart: 1, of which 0 were waited for; matrix products, arithmetic and copies ran while one was open for 0% of the time, Pallas kernels for 26%

profile of v3, /device:TPU:0, one launch (start us, length us, event | category | flops | bytes accessed | tf_op | source)
XLA Modules:
  0.0 158.4 jit_solution(6539608958426887980)
XLA Ops:
  6.5 0.0 all-gather.2.cloned.1.call-start
  6.5 0.6 maximum_bitcast_fusion.freq
  7.1 52.5 %project_plus.1 = (bf16[2,256,512]{2,1,0:T(8,128)(2,1)}, bf16[320,1024]{1,0:T(8,128)(2,1)}, bf16[4,64,1024]{2,1,0:T(8,128)(2,1)}) custom-call(bf16[2,256,1024]{2,1,0:T(8,128)(2,1)} %hidden.3, bf16[4096,512]{1,0:T(8,128)(2,1)} %wq.3, bf16[4096,512]{1,0:T(8,128)(2,1)} %wk.3, bf16[4096,512]{1,0:T(8,128)(2,1)} %wv.3, bf16[512,4096]{1,0:T(8,128)(2,1)} %out_w.1, ...), custom_call_target="tpu_custom_call" | custom-call | tf_op jit(solution)/shard_map/project_plus/pallas_call | solution.py:700
  59.7 0.0 all-gather.2.cloned.1.call-update
  59.7 40.5 %attend_plus.1 = (bf16[2,256,512]{2,1,0:T(8,128)(2,1)}, bf16[320,1024]{1,0:T(8,128)(2,1)}, f32[4,256,128]{2,1,0:T(8,128)}) custom-call(bf16[2,256,1024]{2,1,0:T(8,128)(2,1)} %hidden.3, bf16[4096,512]{1,0:T(8,128)(2,1)} %wq.3, bf16[4096,512]{1,0:T(8,128)(2,1)} %wk.3, bf16[4096,512]{1,0:T(8,128)(2,1)} %wv.3, s32[1,128]{1,0:T(1,128)} %bitcast.6, ...), custom_call_target="tpu_custom_call" | custom-call | tf_op jit(solution)/shard_map/attend_plus/pallas_call | solution.py:714
  100.2 0.0 all-gather.2.cloned.1.call-done.w_in
  100.2 49.4 %attend_minus.1 = bf16[256,1024]{1,0:T(8,128)(2,1)} custom-call(bf16[2,256,512]{2,1,0:T(8,128)(2,1)} %get-tuple-element.13.q_in, bf16[320,1024]{1,0:T(8,128)(2,1)} %get-tuple-element.14.kv_in, s32[1,128]{1,0:T(1,128)} %bitcast.7, f32[4,256,128]{2,1,0:T(8,128)} %get-tuple-element.15.change, bf16[4,512,1024]{2,1,0:T(8,128)(2,1)} %all-gather.2.cloned.1.call-done.w_in), custom_call_target="tpu_custom_call" | custom-call | tf_op jit(solution)/shard_map/attend_minus/pallas_call | solution.py:722
  149.6 1.9 %copy.11 = bf16[256,1024]{1,0:T(8,128)(2,1)} copy(bf16[256,1024]{1,0:T(8,128)(2,1)} %attend_minus.1) | data formatting | bytes 1048576
  (1 shorter events, 0.0 us)
Async XLA Ops:
  6.5 93.7 %all-gather.2.cloned.1.call-start = ((), (), s32[]{:S(2)}) async-start(), calls=%async_computation | async-start | bytes 4718592 | tf_op jit(solution)/shard_map/all_gather | solution.py:713
Sparse Core Ops, SparseCore 0:
  59.8 37.5 all-gather.1

commit v4 on v3

--- a/solution.py
+++ b/solution.py
@@ -18,7 +18,7 @@
 VMEM_LIMIT = 60 * 1024 * 1024
 
 
-def greet(*axes):
+def greet(*axes, all_of=None):
     barrier = pltpu.get_barrier_semaphore()
     peers = 0
     for axis, size in axes:
@@ -33,6 +33,14 @@
             pl.semaphore_signal(barrier, inc=1, device_id={axis: me + 1}, device_id_type=MESH)
 
         peers = peers + jnp.minimum(me, 1) + jnp.minimum(size - 1 - me, 1)
+    if all_of is not None:
+        axis, size = all_of
+        me = lax.axis_index(axis)
+        for shift in range(1, size):
+            pl.semaphore_signal(
+                barrier, inc=1, device_id={axis: (me + shift) % size}, device_id_type=MESH
+            )
+        peers = peers + size - 1
     pl.semaphore_wait(barrier, peers)
 
 
@@ -246,8 +254,10 @@
                         self.has_row > 0.5, placed, base.astype(jnp.float32)
                     ).astype(jnp.bfloat16)
                 else:
-                    kv_out[:, cols] = turned
-        kv_out[:, pl.ds(hw, hw)] = self.acc[:, pl.ds(2 * hw, hw)].astype(jnp.bfloat16)
+                    kv_out[head, :, pl.ds(0, HEAD_DIM)] = turned
+            kv_out[head, :, pl.ds(HEAD_DIM, HEAD_DIM)] = self.acc[
+                :, pl.ds(2 * hw + head * HEAD_DIM, HEAD_DIM)
+            ].astype(jnp.bfloat16)
 
     def drain(self):
         z = self.z
@@ -273,7 +283,8 @@
     def __init__(self, size, slots, strand, q_in, kv_in, sites, work):
         self.size, self.slots, self.strand = size, slots, strand
         self.q_in, self.kv_in = q_in, kv_in
-        self.kvbuf, self.m_buf, self.l_buf, self.a_buf, self.s_sem, self.r_sem = work
+        self.kvbuf, self.kt_buf, self.m_buf, self.l_buf, self.a_buf = work[:5]
+        self.s_sem, self.r_sem = work[5:]
         self.me = lax.axis_index("ctx")
         self.rows, self.hw = q_in.shape[1], q_in.shape[2]
         self.heads = self.hw // HEAD_DIM
@@ -282,80 +293,84 @@
         self.sites_row = sites[...].astype(jnp.float32)
         self.sites_col = to_column(self.sites_row)
 
-    def hop(self, shard, own=False):
+    def hop(self, shard, head, own=False):
         return pltpu.make_async_remote_copy(
-            src_ref=self.kv_in if own else self.kvbuf.at[shard],
-            dst_ref=self.kvbuf.at[shard],
-            send_sem=self.s_sem.at[shard],
-            recv_sem=self.r_sem.at[shard],
+            src_ref=self.kv_in.at[head] if own else self.kvbuf.at[shard, head],
+            dst_ref=self.kvbuf.at[shard, head],
+            send_sem=self.s_sem.at[shard, head],
+            recv_sem=self.r_sem.at[shard, head],
             device_id={"ctx": self.me + 1 if self.strand == 0 else self.me - 1},
             device_id_type=MESH,
         )
 
-    def open(self):
-        @pl.when(self.passes_on)
+    def open(self, head):
+        @pl.when(self.passes_on & (head < self.heads))
         def _():
-            self.hop(self.me, True).start()
+            self.hop(self.me, head, True).start()
 
     def clock(self, place):
         return place if self.strand == 0 else self.window - 1 - place
 
-    def update(self, shard, block, first):
-        rows, hw, slots = self.rows, self.hw, self.slots
+    def times(self):
+        rows, slots = self.rows, self.slots
+
+        def body(shard, carry):
+            begin = (shard * rows).astype(jnp.float32)
+            place = begin + iota((1, rows), 1)
+            _, slot_c = slot_of(self.sites_row, self.sites_col, begin, rows)
+            slot_place, live = slot_row(slot_c, self.sites_col, slots)
+            taken = jnp.sum(
+                jnp.where(self.sites_col == place, 1.0, 0.0), axis=0, keepdims=True
+            )
+            self.kt_buf[shard] = jnp.concatenate(
+                [
+                    jnp.where(taken > 0.5, FAR, self.clock(place)),
+                    jnp.where(live > 0.5, self.clock(slot_place), FAR),
+                ],
+                axis=1,
+            )
+            return carry
+
+        lax.fori_loop(0, self.size, body, 0)
+
+    def update(self, shard, head, block, first):
+        rows, slots = self.rows, self.slots
         q_time = self.clock((self.me * rows).astype(jnp.float32) + iota((rows, 1), 0))
-        begin = (shard * rows).astype(jnp.float32)
-        place = begin + iota((1, rows), 1)
-        ref_time = self.clock(place)
-        _, slot_c = slot_of(self.sites_row, self.sites_col, begin, rows)
-        slot_place, live = slot_row(slot_c, self.sites_col, slots)
-        taken = jnp.sum(jnp.where(self.sites_col == place, 1.0, 0.0), axis=0, keepdims=True)
-        mut_time = jnp.concatenate(
-            [
-                jnp.where(taken > 0.5, FAR, ref_time),
-                jnp.where(live > 0.5, self.clock(slot_place), FAR),
-            ],
-            axis=1,
-        )
-        k_times = (ref_time, mut_time)
+        ref_time = self.clock((shard * rows).astype(jnp.float32) + iota((1, rows), 1))
+        k_times = (ref_time, self.kt_buf[shard])
         spans = (rows, rows + slots)
         log_scale = math.log2(math.e) / math.sqrt(HEAD_DIM)
-
-        def one_head(head, carry):
-            k_cols = pl.ds(pl.multiple_of(head * HEAD_DIM, HEAD_DIM), HEAD_DIM)
-            v_cols = pl.ds(pl.multiple_of(hw + head * HEAD_DIM, HEAD_DIM), HEAD_DIM)
-            for kind in range(2):
-                span = pl.ds(0, spans[kind])
-                raw = lax.dot_general(
-                    self.q_in[kind, :, k_cols],
-                    block[span, k_cols],
-                    (((1,), (1,)), ((), ())),
-                    preferred_element_type=jnp.float32,
-                )
-                raw = jnp.where(k_times[kind] <= q_time, raw, NEG_FILL)
-                top = jnp.max(raw, axis=1, keepdims=True)
-                if not first:
-                    old = self.m_buf[head, kind]
-                    top = jnp.maximum(old, top)
-                    fade = jnp.exp2((old - top) * log_scale)
-                weights = jnp.exp2((raw - top) * log_scale)
-                total = jnp.sum(weights, axis=1, keepdims=True)
-                vec = jnp.dot(
-                    weights.astype(jnp.bfloat16),
-                    block[span, v_cols],
-                    preferred_element_type=jnp.float32,
-                )
-                if not first:
-                    total = total + fade * self.l_buf[head, kind]
-                    vec = vec + fade * self.a_buf[head, kind]
-                self.m_buf[head, kind] = top
-                self.l_buf[head, kind] = total
-                self.a_buf[head, kind] = vec
-            return carry
-
-        lax.fori_loop(0, self.heads, one_head, 0)
-
-    def own_block(self):
-        self.update(self.me, self.kv_in, True)
+        cols = pl.ds(pl.multiple_of(head * HEAD_DIM, HEAD_DIM), HEAD_DIM)
+        for kind in range(2):
+            span = pl.ds(0, spans[kind])
+            raw = lax.dot_general(
+                self.q_in[kind, :, cols],
+                block[span, pl.ds(0, HEAD_DIM)],
+                (((1,), (1,)), ((), ())),
+                preferred_element_type=jnp.float32,
+            )
+            raw = jnp.where(k_times[kind] <= q_time, raw, NEG_FILL)
+            top = jnp.max(raw, axis=1, keepdims=True)
+            if not first:
+                old = self.m_buf[head, kind]
+                top = jnp.maximum(old, top)
+                fade = jnp.exp2((old - top) * log_scale)
+            weights = jnp.exp2((raw - top) * log_scale)
+            total = jnp.sum(weights, axis=1, keepdims=True)
+            vec = jnp.dot(
+                weights.astype(jnp.bfloat16),
+                block[span, pl.ds(HEAD_DIM, HEAD_DIM)],
+                preferred_element_type=jnp.float32,
+            )
+            if not first:
+                total = total + fade * self.l_buf[head, kind]
+                vec = vec + fade * self.a_buf[head, kind]
+            self.m_buf[head, kind] = top
+            self.l_buf[head, kind] = total
+            self.a_buf[head, kind] = vec
+
+    def own_block(self, head):
+        self.update(self.me, head, self.kv_in.at[head], True)
 
     def shard_at(self, step):
         return self.me - step if self.strand == 0 else self.me + step
@@ -364,18 +379,18 @@
         shard = self.shard_at(step)
         return shard >= 0 if self.strand == 0 else shard < self.size
 
-    def arrive(self, step):
+    def arrive(self, step, head):
         shard = self.shard_at(step)
 
         @pl.when(self.alive(step))
         def _():
-            self.hop(shard).wait_recv()
+            self.hop(shard, head).wait_recv()
 
             @pl.when(self.passes_on)
             def _():
-                self.hop(shard).start()
-
-            self.update(shard, self.kvbuf.at[shard], False)
+                self.hop(shard, head).start()
+
+            self.update(shard, head, self.kvbuf.at[shard, head], False)
 
     def change(self, head):
         return self.a_buf[head, 0] / self.l_buf[head, 0] - self.a_buf[head, 1] / self.l_buf[head, 1]
@@ -384,7 +399,8 @@
         def body(step, carry):
             @pl.when(self.alive(step) & self.passes_on)
             def _():
-                self.hop(self.shard_at(step)).wait_send()
+                for head in range(self.heads):
+                    self.hop(self.shard_at(step), head).wait_send()
 
             return carry
 
@@ -489,10 +505,17 @@
     )
     attention = Attention(n_ctx, slots, 0, q_plus, kv_plus, sites, seen)
     layer.open()
-    attention.open()
+    for head in range(attention.heads):
+        attention.open(head)
     loads = layer.load()
     layer.tables()
-    attention.own_block()
+    attention.times()
+
+    def own_head(head, carry):
+        attention.own_block(head)
+        return carry
+
+    lax.fori_loop(0, attention.heads, own_head, 0)
     for copy in loads:
         copy.wait()
 
@@ -503,8 +526,11 @@
         high = jnp.minimum(high, n_ctx)
 
         def body(at, carry):
-            attention.arrive(at)
-            return carry
+            def each(head, inner):
+                attention.arrive(at, head)
+                return inner
+
+            return lax.fori_loop(0, attention.heads, each, carry)
 
         lax.fori_loop(low, high, body, 0)
 
@@ -536,41 +562,39 @@
     *seen,
 ):
     z = lax.axis_index("head")
-    greet(("ctx", n_ctx), ("head", n_head))
+    greet(("ctx", n_ctx), all_of=("head", n_head))
     attention = Attention(n_ctx, slots, 1, q_in, kv_in, sites, seen)
     heads = attention.heads
-    attention.open()
+    attention.open(0)
     w_load = pltpu.make_async_copy(w_in, w_buf, w_sem)
     w_load.start()
-    attention.own_block()
-
-    def body(at, carry):
-        attention.arrive(at)
+    attention.times()
+
+    def deliver(head, peer, source):
+        return pltpu.make_async_remote_copy(
+            src_ref=mine.at[head],
+            dst_ref=gbuf.at[source, head],
+            send_sem=gs_sem.at[peer, head],
+            recv_sem=gr_sem.at[source, head],
+            device_id={"head": peer},
+            device_id_type=MESH,
+        )
+
+    def one_head(head, carry):
+        attention.open(head + 1)
+        attention.own_block(head)
+
+        def body(at, inner):
+            attention.arrive(at, head)
+            return inner
+
+        lax.fori_loop(1, n_ctx, body, 0)
+        mine[head] = (0.5 * (change[head] + attention.change(head))).astype(jnp.bfloat16)
+        for step in range(1, n_head):
+            deliver(head, (z + step) % n_head, z).start()
         return carry
 
-    lax.fori_loop(1, n_ctx, body, 0)
-
-    def pass_on(side, shard, head, own):
-        return pltpu.make_async_remote_copy(
-            src_ref=mine.at[head] if own else gbuf.at[shard, head],
-            dst_ref=gbuf.at[shard, head],
-            send_sem=gs_sem.at[side, shard, head],
-            recv_sem=gr_sem.at[shard, head],
-            device_id={"head": z - 1 if side == 0 else z + 1},
-            device_id_type=MESH,
-        )
-
-    for head in range(heads):
-        mine[head] = (0.5 * (change[head] + attention.change(head))).astype(jnp.bfloat16)
-
-        @pl.when(z > 0)
-        def _():
-            pass_on(0, z, head, True).start()
-
-        @pl.when(z < n_head - 1)
-        def _():
-            pass_on(1, z, head, True).start()
-
+    lax.fori_loop(0, heads, one_head, 0)
     w_load.wait()
 
     def joined(source):
@@ -582,23 +606,7 @@
     def gather_step(step, carry):
         shard = shard_of(step)
         for head in range(heads):
-
-            @pl.when(shard > z)
-            def _():
-                pass_on(0, shard, head, False).wait_recv()
-
-                @pl.when(z > 0)
-                def _():
-                    pass_on(0, shard, head, False).start()
-
-            @pl.when(shard < z)
-            def _():
-                pass_on(1, shard, head, False).wait_recv()
-
-                @pl.when(z < n_head - 1)
-                def _():
-                    pass_on(1, shard, head, False).start()
-
+            deliver(head, shard, shard).wait_recv()
         total_out[...] += jnp.dot(
             joined(gbuf.at[shard]), w_buf[shard], preferred_element_type=jnp.float32
         )
@@ -608,20 +616,11 @@
     out[...] = total_out[...].astype(jnp.bfloat16)
 
     def drain_gather(step, carry):
-        shard = shard_of(step)
         for head in range(heads):
-
-            @pl.when((shard >= z) & (z > 0))
-            def _():
-                pass_on(0, shard, head, False).wait_send()
-
-            @pl.when((shard <= z) & (z < n_head - 1))
-            def _():
-                pass_on(1, shard, head, False).wait_send()
-
+            deliver(head, (z + step) % n_head, z).wait_send()
         return carry
 
-    lax.fori_loop(0, n_head, drain_gather, 0)
+    lax.fori_loop(1, n_head, drain_gather, 0)
     attention.drain()
 
 
@@ -674,15 +673,16 @@
         pltpu.SemaphoreType.DMA((n_head, PIECES)),
     ]
     attend_work = [
-        pltpu.VMEM((n_ctx, wide, 2 * hw), jnp.bfloat16),
+        pltpu.VMEM((n_ctx, heads, wide, 2 * HEAD_DIM), jnp.bfloat16),
+        pltpu.VMEM((n_ctx, 1, wide), jnp.float32),
         pltpu.VMEM((heads, 2, rows, 1), jnp.float32),
         pltpu.VMEM((heads, 2, rows, 1), jnp.float32),
         pltpu.VMEM((heads, 2, rows, HEAD_DIM), jnp.float32),
-        pltpu.SemaphoreType.DMA((n_ctx,)),
-        pltpu.SemaphoreType.DMA((n_ctx,)),
+        pltpu.SemaphoreType.DMA((n_ctx, heads)),
+        pltpu.SemaphoreType.DMA((n_ctx, heads)),
     ]
     q_shape = jax.ShapeDtypeStruct((2, rows, hw), jnp.bfloat16)
-    kv_shape = jax.ShapeDtypeStruct((wide, 2 * hw), jnp.bfloat16)
+    kv_shape = jax.ShapeDtypeStruct((heads, wide, 2 * HEAD_DIM), jnp.bfloat16)
 
     def call(kernel, number, out_shape, in_specs, scratch, name):
         return pl.pallas_call(
@@ -730,7 +730,7 @@
             pltpu.VMEM((heads, rows, HEAD_DIM), jnp.bfloat16),
             pltpu.VMEM((rows, feats), jnp.float32),
             pltpu.SemaphoreType.DMA(()),
-            pltpu.SemaphoreType.DMA((2, n_head, heads)),
+            pltpu.SemaphoreType.DMA((n_head, heads)),
             pltpu.SemaphoreType.DMA((n_head, heads)),
         ]
         + attend_work,

time: 159 us -> 154 us (0.969)
  Pallas kernels: 142 us -> 138 us
    pallas_call x1, Pallas kernels: 49.4 us -> 44.8 us  [shards(): call(functools.partial(last_kernel, n_head, n_ctx, slots), 2, jax.ShapeDt...]
where the time goes in v4:
time: 154 us
  Pallas kernels  138 us (90%)
  between operations  13.4 us (9%)
  local copies, waits for them, and re-layouts  1.87 us (1%)
    pallas_call x1, Pallas kernels, shards(): call(functools.partial(plus_kernel, n_head, slots), 0, (q_shape, kv_shape...  52.5 us
    pallas_call x1, Pallas kernels, shards(): call(functools.partial(last_kernel, n_head, n_ctx, slots), 2, jax.ShapeDt...  44.8 us
    pallas_call x1, Pallas kernels, shards(): call(functools.partial(minus_kernel, n_head, n_ctx, slots), 1, (q_shape,...  40.8 us
  transfers between devices with their start and end apart: 1, of which 0 were waited for; matrix products, arithmetic and copies ran while one was open for 0% of the time, Pallas kernels for 26%

profile of v4, /device:TPU:0, one launch (start us, length us, event | category | flops | bytes accessed | tf_op | source)
XLA Modules:
  0.0 154.1 jit_solution(17664743465709051039)
XLA Ops:
  6.5 0.0 all-gather.2.cloned.1.call-start
  6.5 0.6 maximum_bitcast_fusion.freq
  7.1 52.5 %project_plus.1 = (bf16[2,256,512]{2,1,0:T(8,128)(2,1)}, bf16[4,320,256]{2,1,0:T(8,128)(2,1)}, bf16[4,64,1024]{2,1,0:T(8,128)(2,1)}) custom-call(bf16[2,256,1024]{2,1,0:T(8,128)(2,1)} %hidden.3, bf16[4096,512]{1,0:T(8,128)(2,1)} %wq.3, bf16[4096,512]{1,0:T(8,128)(2,1)} %wk.3, bf16[4096,512]{1,0:T(8,128)(2,1)} %wv.3, bf16[512,4096]{1,0:T(8,128)(2,1)} %out_w.1, ...), custom_call_target="tpu_custom_call" | custom-call | tf_op jit(solution)/shard_map/project_plus/pallas_call | solution.py:700
  59.7 0.0 all-gather.2.cloned.1.call-update
  59.7 40.8 %attend_plus.1 = (bf16[2,256,512]{2,1,0:T(8,128)(2,1)}, bf16[4,320,256]{2,1,0:T(8,128)(2,1)}, f32[4,256,128]{2,1,0:T(8,128)}) custom-call(bf16[2,256,1024]{2,1,0:T(8,128)(2,1)} %hidden.3, bf16[4096,512]{1,0:T(8,128)(2,1)} %wq.3, bf16[4096,512]{1,0:T(8,128)(2,1)} %wk.3, bf16[4096,512]{1,0:T(8,128)(2,1)} %wv.3, s32[1,128]{1,0:T(1,128)} %bitcast.6, ...), custom_call_target="tpu_custom_call" | custom-call | tf_op jit(solution)/shard_map/attend_plus/pallas_call | solution.py:714
  100.5 0.0 all-gather.2.cloned.1.call-done.w_in
  100.5 44.8 %attend_minus.1 = bf16[256,1024]{1,0:T(8,128)(2,1)} custom-call(bf16[2,256,512]{2,1,0:T(8,128)(2,1)} %get-tuple-element.13.q_in, bf16[4,320,256]{2,1,0:T(8,128)(2,1)} %get-tuple-element.14.kv_in, s32[1,128]{1,0:T(1,128)} %bitcast.7, f32[4,256,128]{2,1,0:T(8,128)} %get-tuple-element.15.change, bf16[4,512,1024]{2,1,0:T(8,128)(2,1)} %all-gather.2.cloned.1.call-done.w_in), custom_call_target="tpu_custom_call" | custom-call | tf_op jit(solution)/shard_map/attend_minus/pallas_call | solution.py:722
  145.4 1.9 %copy.11 = bf16[256,1024]{1,0:T(8,128)(2,1)} copy(bf16[256,1024]{1,0:T(8,128)(2,1)} %attend_minus.1) | data formatting | bytes 1048576
  (1 shorter events, 0.0 us)
Async XLA Ops:
  6.5 94.0 %all-gather.2.cloned.1.call-start = ((), (), s32[]{:S(2)}) async-start(), calls=%async_computation | async-start | bytes 4718592 | tf_op jit(solution)/shard_map/all_gather | solution.py:713
Sparse Core Ops, SparseCore 0:
  59.8 37.5 all-gather.1

commit v5 on v4

--- a/solution.py
+++ b/solution.py
@@ -349,19 +349,23 @@
                 (((1,), (1,)), ((), ())),
                 preferred_element_type=jnp.float32,
             )
-            raw = jnp.where(k_times[kind] <= q_time, raw, NEG_FILL)
+            if first:
+                raw = jnp.where(k_times[kind] <= q_time, raw, NEG_FILL)
+            elif kind == 1:
+                raw = raw + jnp.where(k_times[1] >= FAR, NEG_FILL, 0.0)
             top = jnp.max(raw, axis=1, keepdims=True)
             if not first:
                 old = self.m_buf[head, kind]
                 top = jnp.maximum(old, top)
                 fade = jnp.exp2((old - top) * log_scale)
             weights = jnp.exp2((raw - top) * log_scale)
-            total = jnp.sum(weights, axis=1, keepdims=True)
-            vec = jnp.dot(
+            values = block[span, pl.ds(HEAD_DIM, HEAD_DIM)]
+            both = jnp.dot(
                 weights.astype(jnp.bfloat16),
-                block[span, pl.ds(HEAD_DIM, HEAD_DIM)],
+                jnp.concatenate([values, jnp.ones_like(values)], axis=1),
                 preferred_element_type=jnp.float32,
             )
+            vec, total = both[:, :HEAD_DIM], both[:, HEAD_DIM:]
             if not first:
                 total = total + fade * self.l_buf[head, kind]
                 vec = vec + fade * self.a_buf[head, kind]
@@ -676,7 +680,7 @@
         pltpu.VMEM((n_ctx, heads, wide, 2 * HEAD_DIM), jnp.bfloat16),
         pltpu.VMEM((n_ctx, 1, wide), jnp.float32),
         pltpu.VMEM((heads, 2, rows, 1), jnp.float32),
-        pltpu.VMEM((heads, 2, rows, 1), jnp.float32),
+        pltpu.VMEM((heads, 2, rows, HEAD_DIM), jnp.float32),
         pltpu.VMEM((heads, 2, rows, HEAD_DIM), jnp.float32),
         pltpu.SemaphoreType.DMA((n_ctx, heads)),
         pltpu.SemaphoreType.DMA((n_ctx, heads)),

time: 154 us -> 154 us (level)
  no operation moved by 1% of the time
where the time goes in v5:
time: 154 us
  Pallas kernels  138 us (90%)
  between operations  13.4 us (9%)
  local copies, waits for them, and re-layouts  1.87 us (1%)
    pallas_call x1, Pallas kernels, shards(): call(functools.partial(plus_kernel, n_head, slots), 0, (q_shape, kv_shape...  52.5 us
    pallas_call x1, Pallas kernels, shards(): call(functools.partial(last_kernel, n_head, n_ctx, slots), 2, jax.ShapeDt...  45.1 us
    pallas_call x1, Pallas kernels, shards(): call(functools.partial(minus_kernel, n_head, n_ctx, slots), 1, (q_shape,...  40.7 us
  transfers between devices with their start and end apart: 1, of which 0 were waited for; matrix products, arithmetic and copies ran while one was open for 0% of the time, Pallas kernels for 26%

profile of v5, /device:TPU:0, one launch (start us, length us, event | category | flops | bytes accessed | tf_op | source)
XLA Modules:
  0.0 154.2 jit_solution(9437083494645279793)
XLA Ops:
  6.5 0.0 all-gather.2.cloned.1.call-start
  6.5 0.6 maximum_bitcast_fusion.freq
  7.1 52.5 %project_plus.1 = (bf16[2,256,512]{2,1,0:T(8,128)(2,1)}, bf16[4,320,256]{2,1,0:T(8,128)(2,1)}, bf16[4,64,1024]{2,1,0:T(8,128)(2,1)}) custom-call(bf16[2,256,1024]{2,1,0:T(8,128)(2,1)} %hidden.3, bf16[4096,512]{1,0:T(8,128)(2,1)} %wq.3, bf16[4096,512]{1,0:T(8,128)(2,1)} %wk.3, bf16[4096,512]{1,0:T(8,128)(2,1)} %wv.3, bf16[512,4096]{1,0:T(8,128)(2,1)} %out_w.1, ...), custom_call_target="tpu_custom_call" | custom-call | tf_op jit(solution)/shard_map/project_plus/pallas_call | solution.py:704
  59.7 0.0 all-gather.2.cloned.1.call-update
  59.7 40.7 %attend_plus.1 = (bf16[2,256,512]{2,1,0:T(8,128)(2,1)}, bf16[4,320,256]{2,1,0:T(8,128)(2,1)}, f32[4,256,128]{2,1,0:T(8,128)}) custom-call(bf16[2,256,1024]{2,1,0:T(8,128)(2,1)} %hidden.3, bf16[4096,512]{1,0:T(8,128)(2,1)} %wq.3, bf16[4096,512]{1,0:T(8,128)(2,1)} %wk.3, bf16[4096,512]{1,0:T(8,128)(2,1)} %wv.3, s32[1,128]{1,0:T(1,128)} %bitcast.6, ...), custom_call_target="tpu_custom_call" | custom-call | tf_op jit(solution)/shard_map/attend_plus/pallas_call | solution.py:718
  100.4 0.0 all-gather.2.cloned.1.call-done.w_in
  100.4 45.1 %attend_minus.1 = bf16[256,1024]{1,0:T(8,128)(2,1)} custom-call(bf16[2,256,512]{2,1,0:T(8,128)(2,1)} %get-tuple-element.13.q_in, bf16[4,320,256]{2,1,0:T(8,128)(2,1)} %get-tuple-element.14.kv_in, s32[1,128]{1,0:T(1,128)} %bitcast.7, f32[4,256,128]{2,1,0:T(8,128)} %get-tuple-element.15.change, bf16[4,512,1024]{2,1,0:T(8,128)(2,1)} %all-gather.2.cloned.1.call-done.w_in), custom_call_target="tpu_custom_call" | custom-call | tf_op jit(solution)/shard_map/attend_minus/pallas_call | solution.py:726
  145.5 1.9 %copy.11 = bf16[256,1024]{1,0:T(8,128)(2,1)} copy(bf16[256,1024]{1,0:T(8,128)(2,1)} %attend_minus.1) | data formatting | bytes 1048576
  (1 shorter events, 0.0 us)
Async XLA Ops:
  6.5 93.9 %all-gather.2.cloned.1.call-start = ((), (), s32[]{:S(2)}) async-start(), calls=%async_computation | async-start | bytes 4718592 | tf_op jit(solution)/shard_map/all_gather | solution.py:717
Sparse Core Ops, SparseCore 0:
  59.8 37.6 all-gather.1
